TPU v7x, 512 devices: a whole 4x8x8 slice. The times are simulated.
512 devices in a mesh: dp: 16 (over x_lo, z), fsdp: 32 (over x_hi, y, core).
Axes of the slice: x: 4 (x_hi: 2, x_lo: 2; x = x_hi * 2 + x_lo), y: 8, z: 8, core: 2. Of those that a mesh axis runs over, the one named last changes fastest.
Arguments:
- layer_input: bfloat16 [32768, 8192], P('dp', 'fsdp'), may hold values from -6 to 6
- cotangent: bfloat16 [2, 32768, 1024], P(None, ('dp', 'fsdp')), may hold values from -6 to 6
- candidates: bfloat16 [2, 16, 1024, 512], P(None, 'dp', None, 'fsdp'), may hold values from -0.1875 to 0.1875
- moment_first: float32 [2, 512, 8192], P(None, 'dp', 'fsdp'), may hold values from -0.6 to 0.6
- moment_second: float32 [2, 512, 8192], P(None, 'dp', 'fsdp'), may hold values from 0.0001 to 0.01
- owners: int32 [2], replicated, may hold values from 0 to 15
Outputs:
- update: bfloat16 [2, 1024, 8192], P(None, 'dp', 'fsdp')
- first_next: float32 [2, 512, 8192], P(None, 'dp', 'fsdp')
- second_next: float32 [2, 512, 8192], P(None, 'dp', 'fsdp')
Inputs may be any that keep to these rules, and one draw needn't show every extreme that they name: owners[m] names a data-parallel replica.
All inputs are finite; a program needn't handle non-finite values.
Results may differ from a plain program's by a relative error of at most 0.0056.
Values may be sent and summed in bfloat16 or wider, within the bound.
A program may use at most 64 MiB of HBM per device.

v0:
```python
import math

import jax
import jax.numpy as jnp
from jax import lax
from jax.sharding import PartitionSpec as P

MATS = 2
STEP = 10


beta_first = 0.9
beta_second = 0.999
epsilon = 1e-08


def broadcast(x, axis, root):
    return lax.dynamic_index_in_dim(lax.all_gather(x, axis), root, 0, keepdims=False)


def sent_to_all(x, axis):
    count = lax.axis_size(axis)
    return lax.all_to_all(jnp.broadcast_to(x[None], (count, *x.shape)), axis, 0, 0, tiled=True)


def in_order(blocks, dim):
    lengths = list(blocks.shape[1:])
    lengths[dim] *= blocks.shape[0]
    return jnp.moveaxis(blocks, 0, dim).reshape(lengths)


def collect(x, axis, dim):
    blocks = sent_to_all(x, axis)
    return in_order(blocks, dim)


def cut_along(x, dim, count):
    before, after = (x.shape[:dim], x.shape[dim + 1 :])
    return jnp.moveaxis(x.reshape(*before, count, -1, *after), dim, 0)


def summed_on_arrival(x, axis, dim):
    blocks = cut_along(x, dim, lax.axis_size(axis))
    arrived = lax.all_to_all(blocks, axis, split_axis=0, concat_axis=0, tiled=True)
    return arrived.sum(axis=0)


def on_device(layer_input, cotangent, candidates, moment_first, moment_second, owners):
    replicas = lax.axis_size("dp")
    replica_index = lax.axis_index("dp")
    inverse_root = 1.0 / math.sqrt(layer_input.shape[0] * replicas)
    kv_share = candidates.shape[2] // replicas
    updates = []
    firsts = []
    seconds = []
    for matrix in range(MATS):
        candidate_own = candidates[matrix, 0]
        owner_index = owners[matrix]
        owner_block = broadcast(candidate_own, "dp", owner_index)
        projector = collect(owner_block, "fsdp", 1)
        head_rows = jnp.dot(
            cotangent[matrix], projector, preferred_element_type=jnp.float32
        ).astype(jnp.bfloat16)
        partial_value = lax.dot_general(
            lax.all_gather(head_rows, "fsdp", axis=0, tiled=True),
            layer_input,
            (((0,), (0,)), ((), ())),
            preferred_element_type=jnp.float32,
        )
        projected = summed_on_arrival(partial_value, "dp", 0) * inverse_root
        first = beta_first * moment_first[matrix] + (1.0 - beta_first) * projected
        second = beta_second * moment_second[matrix] + (1.0 - beta_second) * projected * projected
        direction = (
            first
            / (1.0 - beta_first**STEP)
            / (jnp.sqrt(second / (1.0 - beta_second**STEP)) + epsilon)
        )
        direction = direction.astype(jnp.bfloat16)
        own_rows = lax.dynamic_slice_in_dim(projector, replica_index * kv_share, kv_share, 0)
        update = jnp.dot(own_rows, collect(direction, "dp", 0), preferred_element_type=jnp.float32)
        updates.append(update.astype(jnp.bfloat16))
        firsts.append(first)
        seconds.append(second)
    return (jnp.stack(updates), jnp.stack(firsts), jnp.stack(seconds))


def solution(mesh):
    placed = (
        P("dp", "fsdp"),
        P(None, ("dp", "fsdp"), None),
        P(None, "dp", None, "fsdp"),
        P(None, "dp", "fsdp"),
        P(None, "dp", "fsdp"),
        P(),
    )
    return jax.shard_map(
        on_device,
        mesh=mesh,
        in_specs=placed,
        out_specs=(P(None, "dp", "fsdp"), P(None, "dp", "fsdp"), P(None, "dp", "fsdp")),
        check_vma=False,
    )
```

profile of v0, /device:TPU:1, one launch (start us, length us, event | category | flops | bytes accessed | tf_op | source)
XLA Modules:
  0.0 324.3 jit_solution(12973515239512783485)
XLA Ops:
  7.2 0.0 copy-start
  7.2 0.0 copy-start.1
  7.2 0.0 all-gather.7.cloned.1.call-start
  7.2 1.4 fusion.15
  9.9 0.8 fusion.14
  10.7 36.5 %all-gather.1 = bf16[16,1,1024,16]{2,3,1,0:T(8,128)(2,1)S(1)} all-gather(bf16[1,1,1024,16]{2,3,1,0:T(8,128)(2,1)S(1)} %get-tuple-element.13), channel_id=3, replica_groups=mesh['dp'=16,'fsdp'=32] {'dp'}, dimensions={0}, use_global_device_ids=true | all-gather | bytes 557056 | tf_op jit(solution)/shard_map/all_gather | solution.py:18
  47.8 0.1 broadcast_in_dim.37
  47.9 43.9 %all_to_all.30 = bf16[32,1024,16]{1,2,0:T(8,128)(2,1)S(1)} all-to-all(bf16[32,1024,16]{1,2,0:T(8,128)(2,1)S(1)} %broadcast_in_dim.37), channel_id=1, replica_groups=mesh['dp'=16,'fsdp'=32] {'fsdp'}, dimensions={0} | all-to-all | bytes 2097152 | tf_op jit(solution)/shard_map/all_to_all | solution.py:23
  91.8 0.0 copy-done.1
  91.8 1.1 fusion.1
  92.9 0.0 all-gather.7.cloned.1.call-update
  92.9 0.0 all-gather.5.cloned.1.call-start
  94.9 25.9 %all-gather = bf16[16,1,1024,16]{2,3,1,0:T(8,128)(2,1)S(1)} all-gather(bf16[1,1,1024,16]{2,3,1,0:T(8,128)(2,1)S(1)} %get-tuple-element.12), channel_id=2, replica_groups=mesh['dp'=16,'fsdp'=32] {'dp'}, dimensions={0}, use_global_device_ids=true | all-gather | bytes 557056 | tf_op jit(solution)/shard_map/all_gather | solution.py:18
  120.8 0.1 broadcast_in_dim.33
  120.9 43.8 %all_to_all.31 = bf16[32,1024,16]{1,2,0:T(8,128)(2,1)S(1)} all-to-all(bf16[32,1024,16]{1,2,0:T(8,128)(2,1)S(1)} %broadcast_in_dim.33), channel_id=1, replica_groups=mesh['dp'=16,'fsdp'=32] {'fsdp'}, dimensions={0} | all-to-all | bytes 2097152 | tf_op jit(solution)/shard_map/all_to_all | solution.py:23
  164.8 1.1 fusion
  165.8 0.0 all-gather.5.cloned.1.call-update
  165.9 9.7 %all-gather.7.cloned.1.call-done = bf16[2048,512]{1,0:T(8,128)(2,1)} async-done(((bf16[64,512]{1,0:T(8,128)(2,1)}), bf16[2048,512]{1,0:T(8,128)(2,1)}) %all-gather.7.cloned.1.call-update) | async-done | bytes 2097168 | tf_op jit(solution)/shard_map/all_gather | solution.py:65
  175.5 0.0 copy-done
  175.5 3.1 fusion.17
  178.7 6.1 %all-to-all-start.4 = ((f32[16,32,256]{2,1,0:T(8,128)}), f32[16,32,256]{2,1,0:T(8,128)}, u32[]{:S(2)}, u32[]{:S(2)}) async-start(f32[16,32,256]{2,1,0:T(8,128)} %bitcast.59), calls=%async_computation.4 | async-start | bytes 1048576 | tf_op jit(solution)/shard_map/all_to_all | solution.py:44
  184.7 0.0 copy-start.2
  184.7 0.0 copy-start.3
  184.8 76.8 %all-gather.5.cloned.1.call-done = bf16[2048,512]{1,0:T(8,128)(2,1)} async-done(((bf16[64,512]{1,0:T(8,128)(2,1)}), bf16[2048,512]{1,0:T(8,128)(2,1)}) %all-gather.5.cloned.1.call-update) | async-done | bytes 2097168 | tf_op jit(solution)/shard_map/all_gather | solution.py:65
  261.6 3.1 fusion.16
  264.7 0.0 all-to-all-done.4
  264.7 7.3 %all-to-all-start.1 = ((f32[16,32,256]{2,1,0:T(8,128)}), f32[16,32,256]{2,1,0:T(8,128)}, u32[]{:S(2)}, u32[]{:S(2)}) async-start(f32[16,32,256]{2,1,0:T(8,128)} %bitcast.58), calls=%async_computation.1 | async-start | bytes 1048576 | tf_op jit(solution)/shard_map/all_to_all | solution.py:44
  272.0 1.1 reduce_sum.19
  273.0 12.6 %all-to-all-done.1 = f32[16,32,256]{2,1,0:T(8,128)} async-done(((f32[16,32,256]{2,1,0:T(8,128)}), f32[16,32,256]{2,1,0:T(8,128)}, u32[]{:S(2)}, u32[]{:S(2)}) %all-to-all-start.1) | async-done | bytes 524320 | tf_op jit(solution)/shard_map/all_to_all | solution.py:44
  285.7 1.1 reduce_sum.18
  286.7 0.0 copy-done.2
  286.8 0.0 copy-done.3
  286.8 0.1 fusion.10
  286.9 15.4 %all_to_all.32 = bf16[16,32,256]{2,1,0:T(8,128)(2,1)} all-to-all(bf16[16,32,256]{2,1,0:T(8,128)(2,1)S(1)} %broadcast_in_dim.35), channel_id=1, replica_groups=mesh['dp'=16,'fsdp'=32] {'dp'}, dimensions={0} | all-to-all | bytes 524288 | tf_op jit(solution)/shard_map/all_to_all | solution.py:23
  302.3 0.7 broadcast_in_dim.39
  303.0 5.6 %all-to-all-start.5 = ((bf16[16,32,256]{2,1,0:T(8,128)(2,1)}), bf16[16,32,256]{2,1,0:T(8,128)(2,1)S(1)}, u32[]{:S(2)}, u32[]{:S(2)}) async-start(bf16[16,32,256]{2,1,0:T(8,128)(2,1)} %broadcast_in_dim.39), calls=%async_computation.5 | async-start | bytes 524288 | tf_op jit(solution)/shard_map/all_to_all | solution.py:23
  308.6 0.7 pad_maximum_fusion.1
  309.3 1.2 fusion.2
  310.5 6.0 %all-to-all-done.5 = bf16[16,32,256]{2,1,0:T(8,128)(2,1)S(1)} async-done(((bf16[16,32,256]{2,1,0:T(8,128)(2,1)}), bf16[16,32,256]{2,1,0:T(8,128)(2,1)S(1)}, u32[]{:S(2)}, u32[]{:S(2)}) %all-to-all-start.5) | async-done | bytes 262176 | tf_op jit(solution)/shard_map/all_to_all | solution.py:23
  316.5 0.3 fusion.3
  316.8 0.6 pad_maximum_fusion
  (3 shorter events, 0.0 us)
Async XLA Ops:
  7.2 168.4 %copy-start = (bf16[2048,256]{1,0:T(8,128)(2,1)S(1)}, bf16[2048,256]{1,0:T(8,128)(2,1)}, u32[]{:S(2)}) copy-start(bf16[2048,256]{1,0:T(8,128)(2,1)} %param.6) | copy-start | bytes 3145732
  7.2 84.6 %copy-start.1 = (bf16[2,64,1024]{2,1,0:T(8,128)(2,1)S(1)}, bf16[2,64,1024]{2,1,0:T(8,128)(2,1)}, u32[]{:S(2)}) copy-start(bf16[2,64,1024]{2,1,0:T(8,128)(2,1)} %param.7) | copy-start | bytes 786436
  7.2 168.3 %all-gather.7.cloned.1.call-start = ((), (), s32[]{:S(2)}) async-start(), calls=%async_computation.7 | async-start | bytes 2162688 | tf_op jit(solution)/shard_map/all_gather | solution.py:65
  92.9 168.6 %all-gather.5.cloned.1.call-start = ((), (), s32[]{:S(2)}) async-start(), calls=%async_computation.6 | async-start | bytes 2162688 | tf_op jit(solution)/shard_map/all_gather | solution.py:65
  178.7 86.0 %all-to-all-start.4 = ((f32[16,32,256]{2,1,0:T(8,128)}), f32[16,32,256]{2,1,0:T(8,128)}, u32[]{:S(2)}, u32[]{:S(2)}) async-start(f32[16,32,256]{2,1,0:T(8,128)} %bitcast.59), calls=%async_computation.4 | async-start | bytes 1048576 | tf_op jit(solution)/shard_map/all_to_all | solution.py:44
  184.7 102.0 %copy-start.2 = (f32[2,32,256]{2,1,0:T(8,128)S(1)}, f32[2,32,256]{2,1,0:T(8,128)}, u32[]{:S(2)}) copy-start(f32[2,32,256]{2,1,0:T(8,128)} %param.9) | copy-start | bytes 196612
  184.7 102.0 %copy-start.3 = (f32[2,32,256]{2,1,0:T(8,128)S(1)}, f32[2,32,256]{2,1,0:T(8,128)}, u32[]{:S(2)}) copy-start(f32[2,32,256]{2,1,0:T(8,128)} %param.10) | copy-start | bytes 196612
  264.7 21.0 %all-to-all-start.1 = ((f32[16,32,256]{2,1,0:T(8,128)}), f32[16,32,256]{2,1,0:T(8,128)}, u32[]{:S(2)}, u32[]{:S(2)}) async-start(f32[16,32,256]{2,1,0:T(8,128)} %bitcast.58), calls=%async_computation.1 | async-start | bytes 1048576 | tf_op jit(solution)/shard_map/all_to_all | solution.py:44
  303.0 13.5 %all-to-all-start.5 = ((bf16[16,32,256]{2,1,0:T(8,128)(2,1)}), bf16[16,32,256]{2,1,0:T(8,128)(2,1)S(1)}, u32[]{:S(2)}, u32[]{:S(2)}) async-start(bf16[16,32,256]{2,1,0:T(8,128)(2,1)} %broadcast_in_dim.39), calls=%async_computation.5 | async-start | bytes 524288 | tf_op jit(solution)/shard_map/all_to_all | solution.py:23
Sparse Core Ops, SparseCore 0:
  93.0 82.4 all-gather.6
  179.4 82.0 all-gather.4
where the time goes:
time: 327 us; the launch traced here: 324 us
  blocking collectives  165 us (50%)
  waiting for transfers between devices  105 us (32%)
  starting transfers between devices  19 us (6%)
  between operations  18.1 us (6%)
  matrix products  9.98 us (3%)
  other arithmetic  3.52 us (1%)
    all_to_all x3, blocking collectives, sent_to_all(): lax.all_to_all(jnp.broadcast_to(x[None], (count, *x.shape)), axis, 0, 0,...  103 us
    all_gather x2, waiting for transfers between devices, on_device(): lax.all_gather(head_rows, 'fsdp', axis=0, tiled=True)  86.5 us
    all_gather x2, blocking collectives, broadcast(): lax.all_gather(x, axis)  62.4 us
    all_to_all x2, starting transfers between devices, summed_on_arrival(): lax.all_to_all(blocks, axis, split_axis=0, concat_axis=0, tiled=True)  13.3 us
    all_to_all x2, waiting for transfers between devices, summed_on_arrival(): lax.all_to_all(blocks, axis, split_axis=0, concat_axis=0, tiled=True)  12.6 us
  transfers between devices with their start and end apart: 5, of which 4 were waited for; matrix products, arithmetic and copies ran while one was open for 3% of the time, Pallas kernels for 0%

commit v1 on v0

v1 whole, which is shorter than its diff:
```python
import math

import jax
import jax.numpy as jnp
from jax import lax
from jax.experimental import pallas as pl
from jax.experimental.pallas import tpu as pltpu
from jax.sharding import PartitionSpec as P

MATS = 2
STEP = 10
TOKENS = 32768
NB = 2
NZ = 8
NA = 2
NY = 8
NC = 2
LANES = 128

beta_first = 0.9
beta_second = 0.999
epsilon = 1e-08

MESH = pl.DeviceIdType.MESH


def kernel(
    owners,
    x_hbm,
    c_hbm,
    cand,
    first_hbm,
    second_hbm,
    update_out,
    first_out,
    second_out,
    xbuf,
    cbuf,
    picked,
    pt,
    ht,
    acc,
    rsend,
    rrecv,
    fsend,
    frecv,
    dirs,
    rows,
    rows_t,
    first_in,
    second_in,
    local_sem,
    x_s,
    x_r,
    c_s,
    c_r,
    pick_s,
    pick_r,
    tile_s,
    tile_r,
    slab_s,
    slab_r,
    rows_s,
    rows_r,
    h_s,
    h_r,
    r_s,
    r_r,
    f_s,
    f_r,
    d_s,
    d_r,
):
    d = lax.axis_index("dp")
    f = lax.axis_index("fsdp")
    b, z = d // NZ, d % NZ
    a, y, c = f // (NY * NC), (f // NC) % NY, f % NC
    own_s = a * NC + c

    def rdma(src, dst, send, recv, dp, fsdp):
        return pltpu.make_async_remote_copy(
            src_ref=src, dst_ref=dst, send_sem=send, recv_sem=recv, device_id=(dp, fsdp), device_id_type=MESH
        )

    def arrived(dst, send, recv):
        rdma(dst, dst, send, recv, d, f).wait_recv()

    def sent(src, send, recv):
        rdma(src, src, send, recv, d, f).wait_send()

    barrier = pltpu.get_barrier_semaphore()

    def greet(dp, fsdp):
        pl.semaphore_signal(barrier, inc=1, device_id=(dp, fsdp), device_id_type=MESH)

    @pl.loop(0, NB * NZ)
    def _(k):
        for core in range(NC):

            @pl.when(jnp.logical_or(k != d, core != c))
            def _():
                greet(k, a * (NY * NC) + y * NC + core)

    for k in range(NB):
        for core in range(NC):
            greet(k * NZ + z, (1 - a) * (NY * NC) + y * NC + core)
    for k in range(1, NY):
        greet(d, a * (NY * NC) + ((y + k) % NY) * NC + c)

    loads = [
        pltpu.make_async_copy(x_hbm, xbuf.at[own_s], local_sem.at[0]),
        pltpu.make_async_copy(c_hbm.at[c], cbuf.at[own_s], local_sem.at[1]),
        pltpu.make_async_copy(first_hbm, first_in, local_sem.at[2]),
        pltpu.make_async_copy(second_hbm, second_in, local_sem.at[3]),
    ]
    for load in loads:
        load.start()
    pl.semaphore_wait(barrier, NB * NZ * NC - 1 + NB * NC + NY - 1)

    def pick_copy(m, k):
        return rdma(
            cand.at[m, :, pl.ds(pl.multiple_of(k * LANES, LANES), LANES)],
            picked.at[d],
            pick_s.at[m * NZ + k],
            pick_r.at[d],
            c * NZ + k,
            a * (NY * NC) + y * NC + m,
        )

    def pick_self(m, k):
        return jnp.logical_and(c == m, c * NZ + k == d)

    for m in range(MATS):

        @pl.loop(0, NZ)
        def _(k, m=m):
            @pl.when(jnp.logical_not(pick_self(m, k)))
            def _():
                pick_copy(m, k).start()

            @pl.when(pick_self(m, k))
            def _():
                pltpu.make_async_copy(
                    cand.at[m, :, pl.ds(pl.multiple_of(k * LANES, LANES), LANES)], picked.at[d], pick_r.at[d]
                ).start()

    trio = ((0, 1), (1, 0), (1, 1))

    def trio_at(i):
        da, dc = trio[i]
        return (a + da) % NA, (c + dc) % NC

    def c_copy(i):
        oa, oc = trio_at(i)
        return rdma(c_hbm.at[oc], cbuf.at[own_s], c_s.at[i], c_r.at[own_s], d, oa * (NY * NC) + y * NC + oc)

    def x_copy(i):
        oa, oc = trio_at(i)
        return rdma(x_hbm, xbuf.at[own_s], x_s.at[i], x_r.at[own_s], d, oa * (NY * NC) + y * NC + oc)

    for i in range(3):
        c_copy(i).start()
    for i in range(3):
        x_copy(i).start()

    @pl.loop(0, NB * NZ)
    def _(k):
        arrived(picked.at[k], pick_s.at[0], pick_r.at[k])

    lanes_own = pl.ds(pl.multiple_of(z * LANES, LANES), LANES)
    pt[y, b, :, lanes_own] = picked[owners[c]]

    def tile_copy(k):
        to = (d + k) % (NB * NZ)
        return rdma(
            pt.at[y, b, :, lanes_own], pt.at[y, b, :, lanes_own], tile_s.at[k], tile_r.at[d], to, f
        )

    @pl.loop(1, NB * NZ)
    def _(k):
        tile_copy(k).start()

    @pl.loop(1, NB * NZ)
    def _(k):
        source = (d + k) % (NB * NZ)
        arrived(
            pt.at[y, source // NZ, :, pl.ds(pl.multiple_of((source % NZ) * LANES, LANES), LANES)],
            tile_s.at[0],
            tile_r.at[source],
        )

    def slab_copy(k):
        return rdma(
            pt.at[y], pt.at[y], slab_s.at[k], slab_r.at[y], d, a * (NY * NC) + ((y + k) % NY) * NC + c
        )

    order = (1, 7, 2, 6, 3, 5, 4)
    for k in order:
        slab_copy(k).start()

    loads[1].wait()
    for i in range(3):
        oa, oc = trio_at(i)
        arrived(cbuf.at[oa * NC + oc], c_s.at[0], c_r.at[oa * NC + oc])
    for k in order:
        source = (y + k) % NY
        arrived(pt.at[source], slab_s.at[0], slab_r.at[source])

    tokens = NA * NC * cbuf.shape[1]
    heads = lax.dot_general(
        pt[...].reshape(NY * NB * 16, NZ * LANES),
        cbuf[...].reshape(tokens, NZ * LANES),
        (((1,), (1,)), ((), ())),
        preferred_element_type=jnp.float32,
    )
    ht[y] = heads.astype(jnp.bfloat16).reshape(2, 128, tokens)

    def ring_copy(way, step, q):
        slot = (y - step + 1) % NY if way == 0 else (y + step - 1) % NY
        to = (y + 1) % NY if way == 0 else (y + NY - 1) % NY
        return rdma(
            ht.at[slot, q],
            ht.at[slot, q],
            h_s.at[way, step - 1, q],
            h_r.at[way, step - 1, q],
            d,
            a * (NY * NC) + to * NC + c,
        )

    def ring_slot(way, step):
        return (y - step + NY) % NY if way == 0 else (y + step) % NY

    def ring_arrived(way, step, q):
        arrived(ht.at[ring_slot(way, step), q], h_s.at[0, 0, 0], h_r.at[way, step - 1, q])

    def forward(step):
        for q in range(2):
            for way in range(2):
                if step > 1:
                    ring_arrived(way, step - 1, q)
                if step < 4 or q == way:
                    ring_copy(way, step, q).start()

    def product(slots, start):
        for s in range(NA * NC):
            total = None if start else acc[s]
            for slot in slots:
                part = jnp.dot(
                    ht[slot].reshape(256, tokens),
                    xbuf[s, :, slot].reshape(tokens, 256),
                    preferred_element_type=jnp.float32,
                )
                total = part if total is None else total + part
            acc[s] = total

    def rows_copy(i):
        oa, oc = trio_at(i)
        return rdma(
            pt.at[:, :, :, pl.ds(pl.multiple_of((d // 2) * LANES, LANES), LANES)],
            rows.at[c, a],
            rows_s.at[i],
            rows_r.at[own_s],
            d,
            oa * (NY * NC) + y * NC + oc,
        )

    forward(1)
    for i in range(3):
        rows_copy(i).start()
    rows[c, a] = pt[:, :, :, pl.ds(pl.multiple_of((d // 2) * LANES, LANES), LANES)]
    forward(2)
    loads[0].wait()
    for i in range(3):
        oa, oc = trio_at(i)
        arrived(xbuf.at[oa * NC + oc], x_s.at[0], x_r.at[oa * NC + oc])
    product((y, ring_slot(0, 1), ring_slot(1, 1)), True)
    forward(3)
    product((ring_slot(0, 2), ring_slot(1, 2)), False)
    forward(4)
    product((ring_slot(0, 3), ring_slot(1, 3)), False)
    ring_arrived(0, 4, 0)
    ring_arrived(1, 4, 1)
    product((ring_slot(0, 4),), False)

    for k in range(NZ):
        for s in range(NA * NC):
            rsend[k, s] = acc[s, 32 * k : 32 * k + 32, :].astype(jnp.bfloat16)

    def r_copy(k):
        to = (z + k) % NZ
        return rdma(rsend.at[to], rrecv.at[z], r_s.at[k], r_r.at[z], b * NZ + to, f)

    for k in (4, 3, 5, 2, 6, 1, 7):
        r_copy(k).start()
    for i in range(3):
        oa, oc = trio_at(i)
        arrived(rows.at[oc, oa], rows_s.at[0], rows_r.at[oa * NC + oc])
    for m in range(MATS):
        rows_t[m] = rows[m].reshape(512, LANES).T
    loads[2].wait()
    loads[3].wait()
    total = rsend[z].astype(jnp.float32)
    for k in order:
        source = (z + k) % NZ
        arrived(rrecv.at[source], r_s.at[0], r_r.at[source])
        total = total + rrecv[source].astype(jnp.float32)
    fsend[...] = total.astype(jnp.bfloat16)

    def f_self(s):
        return jnp.logical_and(s == own_s, a == b)

    def f_copy(s):
        return rdma(
            fsend.at[s],
            frecv.at[b, c],
            f_s.at[s],
            f_r.at[b * NC + c],
            a * NZ + z,
            (s // NC) * (NY * NC) + y * NC + s % NC,
        )

    for s in range(NA * NC):

        @pl.when(jnp.logical_not(f_self(s)))
        def _(s=s):
            f_copy(s).start()

        @pl.when(f_self(s))
        def _(s=s):
            pltpu.make_async_copy(fsend.at[s], frecv.at[b, c], f_r.at[b * NC + c]).start()

    for k in range(NB):
        for m in range(NC):
            arrived(frecv.at[k, m], f_s.at[0], f_r.at[k * NC + m])

    inverse_root = 1.0 / math.sqrt(TOKENS)
    projected = (frecv[0].astype(jnp.float32) + frecv[1].astype(jnp.float32)) * inverse_root
    first = beta_first * first_in[...] + (1.0 - beta_first) * projected
    second = beta_second * second_in[...] + (1.0 - beta_second) * projected * projected
    direction = (
        first / (1.0 - beta_first**STEP) / (jnp.sqrt(second / (1.0 - beta_second**STEP)) + epsilon)
    )
    dirs[d] = direction.astype(jnp.bfloat16)

    def d_copy(k):
        return rdma(dirs.at[d], dirs.at[d], d_s.at[k], d_r.at[d], (d + k) % (NB * NZ), f)

    @pl.loop(1, NB * NZ)
    def _(k):
        d_copy(k).start()

    first_out[...] = first
    second_out[...] = second

    @pl.loop(1, NB * NZ)
    def _(k):
        source = (d + k) % (NB * NZ)
        arrived(dirs.at[source], d_s.at[0], d_r.at[source])

    for m in range(MATS):
        update_out[m] = jnp.dot(
            rows_t[m, pl.ds(pl.multiple_of((d % 2) * 64, 64), 64), :],
            dirs[:, m].reshape(512, 256),
            preferred_element_type=jnp.float32,
        ).astype(jnp.bfloat16)

    for m in range(MATS):

        @pl.loop(0, NZ)
        def _(k, m=m):
            @pl.when(jnp.logical_not(pick_self(m, k)))
            def _():
                pick_copy(m, k).wait_send()

    for i in range(3):
        c_copy(i).wait_send()
        x_copy(i).wait_send()
        rows_copy(i).wait_send()

    @pl.loop(1, NB * NZ)
    def _(k):
        tile_copy(k).wait_send()
        d_copy(k).wait_send()

    for k in order:
        slab_copy(k).wait_send()
        r_copy(k).wait_send()
    for step in range(1, 5):
        for q in range(2):
            for way in range(2):
                if step < 4 or q == way:
                    ring_copy(way, step, q).wait_send()
    for s in range(NA * NC):

        @pl.when(jnp.logical_not(f_self(s)))
        def _(s=s):
            f_copy(s).wait_send()


def on_device(layer_input, cotangent, candidates, moment_first, moment_second, owners):
    bf16, f32 = jnp.bfloat16, jnp.float32
    x = layer_input.reshape(NA, NY, 128, 256)
    cand = jnp.swapaxes(candidates[:, 0], 1, 2)
    vmem = pl.BlockSpec(memory_space=pltpu.VMEM)
    hbm = pl.BlockSpec(memory_space=pl.ANY)
    sem = pltpu.SemaphoreType.DMA
    return pl.pallas_call(
        kernel,
        out_shape=(
            jax.ShapeDtypeStruct((MATS, 64, 256), bf16),
            jax.ShapeDtypeStruct((MATS, 32, 256), f32),
            jax.ShapeDtypeStruct((MATS, 32, 256), f32),
        ),
        in_specs=[pl.BlockSpec(memory_space=pltpu.SMEM), hbm, hbm, hbm, hbm, hbm],
        out_specs=(vmem, vmem, vmem),
        scratch_shapes=[
            pltpu.VMEM((4, NA, NY, 128, 256), bf16),
            pltpu.VMEM((4, 64, 1024), bf16),
            pltpu.VMEM((16, 16, LANES), bf16),
            pltpu.VMEM((NY, NB, 16, 1024), bf16),
            pltpu.VMEM((NY, 2, 128, 256), bf16),
            pltpu.VMEM((4, 256, 256), f32),
            pltpu.VMEM((NZ, 4, 32, 256), bf16),
            pltpu.VMEM((NZ, 4, 32, 256), bf16),
            pltpu.VMEM((4, 32, 256), bf16),
            pltpu.VMEM((NB, MATS, 32, 256), bf16),
            pltpu.VMEM((16, MATS, 32, 256), bf16),
            pltpu.VMEM((MATS, NA, NY, NB, 16, LANES), bf16),
            pltpu.VMEM((MATS, LANES, 512), bf16),
            pltpu.VMEM((MATS, 32, 256), f32),
            pltpu.VMEM((MATS, 32, 256), f32),
            sem((4,)),
            sem((3,)),
            sem((4,)),
            sem((3,)),
            sem((4,)),
            sem((16,)),
            sem((16,)),
            sem((16,)),
            sem((16,)),
            sem((NY,)),
            sem((NY,)),
            sem((3,)),
            sem((4,)),
            sem((2, 4, 2)),
            sem((2, 4, 2)),
            sem((NZ,)),
            sem((NZ,)),
            sem((4,)),
            sem((4,)),
            sem((16,)),
            sem((16,)),
        ],
        compiler_params=pltpu.CompilerParams(
            collective_id=0, has_side_effects=True, vmem_limit_bytes=67043328
        ),
    )(owners, x, cotangent, cand, moment_first, moment_second)


def solution(mesh):
    placed = (
        P("dp", "fsdp"),
        P(None, ("dp", "fsdp"), None),
        P(None, "dp", None, "fsdp"),
        P(None, "dp", "fsdp"),
        P(None, "dp", "fsdp"),
        P(),
    )
    return jax.shard_map(
        on_device,
        mesh=mesh,
        in_specs=placed,
        out_specs=(P(None, "dp", "fsdp"), P(None, "dp", "fsdp"), P(None, "dp", "fsdp")),
        check_vma=False,
    )
```

time: 327 us -> 134 us (0.41)
  blocking collectives: 165 us -> 0 us
  Pallas kernels: 0 us -> 128 us
  waiting for transfers between devices: 105 us -> 0 us
  starting transfers between devices: 19 us -> 0 us
  between operations: 18.1 us -> 0.65 us
  matrix products: 9.98 us -> 0 us
  other arithmetic: 3.52 us -> 0 us
    pallas_call x0 -> x1, Pallas kernels: none -> 128 us  [on_device(): pl.pallas_call(kernel, out_shape=(jax.ShapeDtypeStruct((MATS, 64, 256), b...]
    all_to_all x3 -> x0, blocking collectives: 103 us -> none  [sent_to_all(): lax.all_to_all(jnp.broadcast_to(x[None], (count, *x.shape)), axis, 0, 0,...]
    all_gather x2 -> x0, waiting for transfers between devices: 86.5 us -> none  [on_device(): lax.all_gather(head_rows, 'fsdp', axis=0, tiled=True)]
    all_gather x2 -> x0, blocking collectives: 62.4 us -> none  [broadcast(): lax.all_gather(x, axis)]
    all_to_all x3 -> x0, starting transfers between devices: 18.9 us -> none  [the longest x2 13.3 us: summed_on_arrival(): lax.all_to_all(blocks, axis, split_axis=0, concat_axis=0, tiled=True)]
    all_to_all x3 -> x0, waiting for transfers between devices: 18.6 us -> none  [the longest x2 12.6 us: summed_on_arrival(): lax.all_to_all(blocks, axis, split_axis=0, concat_axis=0, tiled=True)]
    dot_general x6 -> x0, matrix products: 9.98 us -> none  [the longest x2 6.28 us: on_device(): lax.dot_general(lax.all_gather(head_rows, 'fsdp', axis=0, tiled=True), la...]
  transfers between devices with their start and end apart: 5 -> 0, of which waited for: 4 -> 0; matrix products, arithmetic and copies ran while one was open for 3% -> 0% of each run, Pallas kernels for 0% -> 0%
where the time goes in v1:
time: 134 us; the launch traced here: 131 us
  Pallas kernels  128 us (96%)
  local copies, waits for them, and re-layouts  3 us (2%)
    pallas_call x1, Pallas kernels, on_device(): pl.pallas_call(kernel, out_shape=(jax.ShapeDtypeStruct((MATS, 64, 256), b...  128 us
    unnamed x7, local copies, waits for them, and re-layouts  3 us

profile of v1, /device:TPU:1, one launch (start us, length us, event | category | flops | bytes accessed | tf_op | source)
XLA Modules:
  0.0 131.5 jit_solution(2965355963359610917)
XLA Ops:
  0.6 127.8 %shard_map.85 = (bf16[2,64,256]{2,1,0:T(8,128)(2,1)}, f32[2,32,256]{2,1,0:T(8,128)}, f32[2,32,256]{2,1,0:T(8,128)}) custom-call(s32[2]{0:T(128)} %owners.1, bf16[2,8,128,256]{3,2,1,0:T(8,128)(2,1)} %bitcast.4, bf16[2,64,1024]{2,1,0:T(8,128)(2,1)} %c_hbm.1, bf16[2,16,1024]{2,1,0:T(8,128)(2,1)} %bitcast.5, f32[2,32,256]{2,1,0:T(8,128)} %first_hbm.1, ...), custom_call_target="tpu_custom_call" | custom-call | tf_op jit(solution)/shard_map/pallas_call | solution.py:407
  128.5 0.0 copy-start.1
  128.5 1.5 %copy.12 = bf16[2,64,256]{2,1,0:T(8,128)(2,1)} copy(bf16[2,64,256]{2,1,0:T(8,128)(2,1)} %get-tuple-element.6) | data formatting | bytes 131072
  130.0 0.0 copy-done.1
  130.0 0.0 copy-start
  130.0 0.6 copy.13
  130.6 0.2 copy-done
  130.8 0.6 copy.14
Async XLA Ops:
  128.5 1.5 %copy-start.1 = (f32[2,32,256]{2,1,0:T(8,128)S(1)}, f32[2,32,256]{2,1,0:T(8,128)}, u32[]{:S(2)}) copy-start(f32[2,32,256]{2,1,0:T(8,128)} %get-tuple-element.7) | copy-start | bytes 196612
  130.0 0.9 copy-start

commit v2 on v1

--- a/solution.py
+++ b/solution.py
@@ -89,6 +89,7 @@
         rdma(src, src, send, recv, d, f).wait_send()
 
     barrier = pltpu.get_barrier_semaphore()
+    leaving = []
 
     def greet(dp, fsdp):
         pl.semaphore_signal(barrier, inc=1, device_id=(dp, fsdp), device_id_type=MESH)
@@ -119,30 +120,39 @@
 
     def pick_copy(m, k):
         return rdma(
-            cand.at[m, :, pl.ds(pl.multiple_of(k * LANES, LANES), LANES)],
-            picked.at[d],
-            pick_s.at[m * NZ + k],
-            pick_r.at[d],
-            c * NZ + k,
+            cand.at[m, :, pl.ds(pl.multiple_of((k % NZ) * LANES, LANES), LANES)],
+            picked.at[d, c],
+            pick_s.at[m, k],
+            pick_r.at[d, c],
+            k,
             a * (NY * NC) + y * NC + m,
         )
 
     def pick_self(m, k):
-        return jnp.logical_and(c == m, c * NZ + k == d)
+        return jnp.logical_and(c == m, k == d)
 
     for m in range(MATS):
 
-        @pl.loop(0, NZ)
+        @pl.loop(0, NB * NZ)
         def _(k, m=m):
             @pl.when(jnp.logical_not(pick_self(m, k)))
             def _():
                 pick_copy(m, k).start()
 
-            @pl.when(pick_self(m, k))
-            def _():
-                pltpu.make_async_copy(
-                    cand.at[m, :, pl.ds(pl.multiple_of(k * LANES, LANES), LANES)], picked.at[d], pick_r.at[d]
-                ).start()
+    lanes_own = pl.ds(pl.multiple_of(z * LANES, LANES), LANES)
+    pick_own = pltpu.make_async_copy(cand.at[c, :, lanes_own], picked.at[d, c], pick_r.at[d, c])
+    pick_own.start()
+
+    def picks_left():
+        for m in range(MATS):
+
+            @pl.loop(0, NB * NZ)
+            def _(k, m=m):
+                @pl.when(jnp.logical_not(pick_self(m, k)))
+                def _():
+                    pick_copy(m, k).wait_send()
+
+    leaving.append(picks_left)
 
     trio = ((0, 1), (1, 0), (1, 1))
 
@@ -154,49 +164,75 @@
         oa, oc = trio_at(i)
         return rdma(c_hbm.at[oc], cbuf.at[own_s], c_s.at[i], c_r.at[own_s], d, oa * (NY * NC) + y * NC + oc)
 
-    def x_copy(i):
-        oa, oc = trio_at(i)
-        return rdma(x_hbm, xbuf.at[own_s], x_s.at[i], x_r.at[own_s], d, oa * (NY * NC) + y * NC + oc)
+    def x_copy(half, away):
+        oa, oc = (1 - a, c) if away else (a, 1 - c)
+        return rdma(
+            x_hbm.at[half],
+            xbuf.at[own_s, half],
+            x_s.at[half, away],
+            x_r.at[own_s, half],
+            d,
+            oa * (NY * NC) + y * NC + oc,
+        )
+
+    far_s = (1 - a) * NC + c
+
+    def x_pass(half):
+        return rdma(
+            xbuf.at[far_s, half],
+            xbuf.at[far_s, half],
+            x_s.at[half, 2],
+            x_r.at[far_s, half],
+            d,
+            a * (NY * NC) + y * NC + 1 - c,
+        )
 
     for i in range(3):
         c_copy(i).start()
-    for i in range(3):
-        x_copy(i).start()
-
-    @pl.loop(0, NB * NZ)
-    def _(k):
-        arrived(picked.at[k], pick_s.at[0], pick_r.at[k])
-
-    lanes_own = pl.ds(pl.multiple_of(z * LANES, LANES), LANES)
-    pt[y, b, :, lanes_own] = picked[owners[c]]
+        leaving.append(c_copy(i).wait_send)
+    for half in range(NA):
+        x_copy(half, 1).start()
+        leaving.append(x_copy(half, 1).wait_send)
+    for half in range(NA):
+        x_copy(half, 0).start()
+        leaving.append(x_copy(half, 0).wait_send)
+
+    for core in range(NC):
+
+        @pl.loop(0, NB * NZ)
+        def _(k, core=core):
+            arrived(picked.at[k, core], pick_s.at[0, 0], pick_r.at[k, core])
+
+    pt[y, :, :, lanes_own] = picked[owners[c]]
 
     def tile_copy(k):
-        to = (d + k) % (NB * NZ)
-        return rdma(
-            pt.at[y, b, :, lanes_own], pt.at[y, b, :, lanes_own], tile_s.at[k], tile_r.at[d], to, f
-        )
-
-    @pl.loop(1, NB * NZ)
-    def _(k):
-        tile_copy(k).start()
-
-    @pl.loop(1, NB * NZ)
-    def _(k):
-        source = (d + k) % (NB * NZ)
-        arrived(
-            pt.at[y, source // NZ, :, pl.ds(pl.multiple_of((source % NZ) * LANES, LANES), LANES)],
-            tile_s.at[0],
-            tile_r.at[source],
-        )
-
-    def slab_copy(k):
-        return rdma(
-            pt.at[y], pt.at[y], slab_s.at[k], slab_r.at[y], d, a * (NY * NC) + ((y + k) % NY) * NC + c
+        return rdma(
+            pt.at[y, :, :, lanes_own],
+            pt.at[y, :, :, lanes_own],
+            tile_s.at[k],
+            tile_r.at[z],
+            b * NZ + (z + k) % NZ,
+            f,
         )
 
     order = (1, 7, 2, 6, 3, 5, 4)
     for k in order:
+        tile_copy(k).start()
+        leaving.append(tile_copy(k).wait_send)
+    for k in order:
+        source = (z + k) % NZ
+        arrived(
+            pt.at[y, :, :, pl.ds(pl.multiple_of(source * LANES, LANES), LANES)], tile_s.at[0], tile_r.at[source]
+        )
+
+    def slab_copy(k):
+        return rdma(
+            pt.at[y], pt.at[y], slab_s.at[k], slab_r.at[y], d, a * (NY * NC) + ((y + k) % NY) * NC + c
+        )
+
+    for k in order:
         slab_copy(k).start()
+        leaving.append(slab_copy(k).wait_send)
 
     loads[1].wait()
     for i in range(3):
@@ -240,6 +276,7 @@
                     ring_arrived(way, step - 1, q)
                 if step < 4 or q == way:
                     ring_copy(way, step, q).start()
+                    leaving.append(ring_copy(way, step, q).wait_send)
 
     def product(slots, start):
         for s in range(NA * NC):
@@ -267,17 +304,21 @@
     forward(1)
     for i in range(3):
         rows_copy(i).start()
+        leaving.append(rows_copy(i).wait_send)
     rows[c, a] = pt[:, :, :, pl.ds(pl.multiple_of((d // 2) * LANES, LANES), LANES)]
+    for half in range(NA):
+        arrived(xbuf.at[far_s, half], x_s.at[0, 0], x_r.at[far_s, half])
+        x_pass(half).start()
+        leaving.append(x_pass(half).wait_send)
     forward(2)
+    forward(3)
     loads[0].wait()
-    for i in range(3):
-        oa, oc = trio_at(i)
-        arrived(xbuf.at[oa * NC + oc], x_s.at[0], x_r.at[oa * NC + oc])
+    for half in range(NA):
+        for from_s in (a * NC + 1 - c, (1 - a) * NC + 1 - c):
+            arrived(xbuf.at[from_s, half], x_s.at[0, 0], x_r.at[from_s, half])
     product((y, ring_slot(0, 1), ring_slot(1, 1)), True)
-    forward(3)
-    product((ring_slot(0, 2), ring_slot(1, 2)), False)
     forward(4)
-    product((ring_slot(0, 3), ring_slot(1, 3)), False)
+    product((ring_slot(0, 2), ring_slot(1, 2), ring_slot(0, 3), ring_slot(1, 3)), False)
     ring_arrived(0, 4, 0)
     ring_arrived(1, 4, 1)
     product((ring_slot(0, 4),), False)
@@ -292,6 +333,7 @@
 
     for k in (4, 3, 5, 2, 6, 1, 7):
         r_copy(k).start()
+        leaving.append(r_copy(k).wait_send)
     for i in range(3):
         oa, oc = trio_at(i)
         arrived(rows.at[oc, oa], rows_s.at[0], rows_r.at[oa * NC + oc])
@@ -329,6 +371,15 @@
         def _(s=s):
             pltpu.make_async_copy(fsend.at[s], frecv.at[b, c], f_r.at[b * NC + c]).start()
 
+    def f_left():
+        for s in range(NA * NC):
+
+            @pl.when(jnp.logical_not(f_self(s)))
+            def _(s=s):
+                f_copy(s).wait_send()
+
+    leaving.append(f_left)
+
     for k in range(NB):
         for m in range(NC):
             arrived(frecv.at[k, m], f_s.at[0], f_r.at[k * NC + m])
@@ -349,6 +400,13 @@
     def _(k):
         d_copy(k).start()
 
+    def dirs_left():
+        @pl.loop(1, NB * NZ)
+        def _(k):
+            d_copy(k).wait_send()
+
+    leaving.append(dirs_left)
+
     first_out[...] = first
     second_out[...] = second
 
@@ -364,37 +422,8 @@
             preferred_element_type=jnp.float32,
         ).astype(jnp.bfloat16)
 
-    for m in range(MATS):
-
-        @pl.loop(0, NZ)
-        def _(k, m=m):
-            @pl.when(jnp.logical_not(pick_self(m, k)))
-            def _():
-                pick_copy(m, k).wait_send()
-
-    for i in range(3):
-        c_copy(i).wait_send()
-        x_copy(i).wait_send()
-        rows_copy(i).wait_send()
-
-    @pl.loop(1, NB * NZ)
-    def _(k):
-        tile_copy(k).wait_send()
-        d_copy(k).wait_send()
-
-    for k in order:
-        slab_copy(k).wait_send()
-        r_copy(k).wait_send()
-    for step in range(1, 5):
-        for q in range(2):
-            for way in range(2):
-                if step < 4 or q == way:
-                    ring_copy(way, step, q).wait_send()
-    for s in range(NA * NC):
-
-        @pl.when(jnp.logical_not(f_self(s)))
-        def _(s=s):
-            f_copy(s).wait_send()
+    for wait in leaving:
+        wait()
 
 
 def on_device(layer_input, cotangent, candidates, moment_first, moment_second, owners):
@@ -416,7 +445,7 @@
         scratch_shapes=[
             pltpu.VMEM((4, NA, NY, 128, 256), bf16),
             pltpu.VMEM((4, 64, 1024), bf16),
-            pltpu.VMEM((16, 16, LANES), bf16),
+            pltpu.VMEM((16, NC, 16, LANES), bf16),
             pltpu.VMEM((NY, NB, 16, 1024), bf16),
             pltpu.VMEM((NY, 2, 128, 256), bf16),
             pltpu.VMEM((4, 256, 256), f32),
@@ -430,14 +459,14 @@
             pltpu.VMEM((MATS, 32, 256), f32),
             pltpu.VMEM((MATS, 32, 256), f32),
             sem((4,)),
+            sem((NA, 3)),
+            sem((4, NA)),
             sem((3,)),
             sem((4,)),
-            sem((3,)),
-            sem((4,)),
-            sem((16,)),
-            sem((16,)),
-            sem((16,)),
-            sem((16,)),
+            sem((MATS, 16)),
+            sem((16, NC)),
+            sem((NZ,)),
+            sem((NZ,)),
             sem((NY,)),
             sem((NY,)),
             sem((3,)),

time: 134 us -> 95.9 us (0.72); the launches traced: 131 us -> 95.2 us
  Pallas kernels: 128 us -> 91.5 us
    pallas_call x1, Pallas kernels: 128 us -> 91.5 us  [on_device(): pl.pallas_call(kernel, out_shape=(jax.ShapeDtypeStruct((MATS, 64, 256), b...]
where the time goes in v2:
time: 95.9 us; the launch traced here: 95.2 us
  Pallas kernels  91.5 us (95%)
  local copies, waits for them, and re-layouts  3 us (3%)
    pallas_call x1, Pallas kernels, on_device(): pl.pallas_call(kernel, out_shape=(jax.ShapeDtypeStruct((MATS, 64, 256), b...  91.5 us
    unnamed x7, local copies, waits for them, and re-layouts  3 us

profile of v2, /device:TPU:1, one launch (start us, length us, event | category | flops | bytes accessed | tf_op | source)
XLA Modules:
  0.0 95.2 jit_solution(1774478202355349057)
XLA Ops:
  0.6 91.5 %shard_map.85 = (bf16[2,64,256]{2,1,0:T(8,128)(2,1)}, f32[2,32,256]{2,1,0:T(8,128)}, f32[2,32,256]{2,1,0:T(8,128)}) custom-call(s32[2]{0:T(128)} %owners.1, bf16[2,8,128,256]{3,2,1,0:T(8,128)(2,1)} %bitcast.4, bf16[2,64,1024]{2,1,0:T(8,128)(2,1)} %c_hbm.1, bf16[2,16,1024]{2,1,0:T(8,128)(2,1)} %bitcast.5, f32[2,32,256]{2,1,0:T(8,128)} %first_hbm.1, ...), custom_call_target="tpu_custom_call" | custom-call | tf_op jit(solution)/shard_map/pallas_call | solution.py:436
  92.2 0.0 copy-start.1
  92.2 1.5 %copy.12 = bf16[2,64,256]{2,1,0:T(8,128)(2,1)} copy(bf16[2,64,256]{2,1,0:T(8,128)(2,1)} %get-tuple-element.6) | data formatting | bytes 131072
  93.7 0.0 copy-done.1
  93.7 0.0 copy-start
  93.7 0.6 copy.13
  94.3 0.2 copy-done
  94.5 0.6 copy.14
Async XLA Ops:
  92.2 1.5 %copy-start.1 = (f32[2,32,256]{2,1,0:T(8,128)S(1)}, f32[2,32,256]{2,1,0:T(8,128)}, u32[]{:S(2)}) copy-start(f32[2,32,256]{2,1,0:T(8,128)} %get-tuple-element.7) | copy-start | bytes 196612
  93.7 0.9 copy-start

commit v3 on v2

v3 whole, which is shorter than its diff:
```python
import math

import jax
import jax.numpy as jnp
from jax import lax
from jax.experimental import pallas as pl
from jax.experimental.pallas import tpu as pltpu
from jax.sharding import PartitionSpec as P

MATS = 2
STEP = 10
TOKENS = 32768
NB = 2
NZ = 8
NA = 2
NY = 8
NC = 2
LANES = 128

beta_first = 0.9
beta_second = 0.999
epsilon = 1e-08

MESH = pl.DeviceIdType.MESH


def kernel(
    owners,
    x_hbm,
    c_hbm,
    cand,
    first_hbm,
    second_hbm,
    update_out,
    first_out,
    second_out,
    xbuf,
    cbuf,
    picked,
    pt,
    ht,
    acc,
    rsend,
    rrecv,
    fsend,
    frecv,
    dirs,
    rows,
    rows_t,
    first_in,
    second_in,
    local_sem,
    x_s,
    x_r,
    c_s,
    c_r,
    pick_s,
    pick_r,
    tile_s,
    tile_r,
    slab_s,
    slab_r,
    rows_s,
    rows_r,
    h_s,
    h_r,
    r_s,
    r_r,
    f_s,
    f_r,
    d_s,
    d_r,
    p_s,
):
    d = lax.axis_index("dp")
    f = lax.axis_index("fsdp")
    b, z = d // NZ, d % NZ
    a, y, c = f // (NY * NC), (f // NC) % NY, f % NC
    own_s = a * NC + c

    def rdma(src, dst, send, recv, dp, fsdp):
        return pltpu.make_async_remote_copy(
            src_ref=src, dst_ref=dst, send_sem=send, recv_sem=recv, device_id=(dp, fsdp), device_id_type=MESH
        )

    def arrived(dst, send, recv):
        rdma(dst, dst, send, recv, d, f).wait_recv()

    def sent(src, send, recv):
        rdma(src, src, send, recv, d, f).wait_send()

    barrier = pltpu.get_barrier_semaphore()
    leaving = []

    def greet(dp, fsdp):
        pl.semaphore_signal(barrier, inc=1, device_id=(dp, fsdp), device_id_type=MESH)

    @pl.loop(0, NB * NZ)
    def _(k):
        for core in range(NC):

            @pl.when(jnp.logical_or(k != d, core != c))
            def _():
                greet(k, a * (NY * NC) + y * NC + core)

    for k in range(NB):
        for core in range(NC):
            greet(k * NZ + z, (1 - a) * (NY * NC) + y * NC + core)
    for k in range(1, NY):
        greet(d, a * (NY * NC) + ((y + k) % NY) * NC + c)

    loads = [
        pltpu.make_async_copy(x_hbm, xbuf.at[own_s], local_sem.at[0]),
        pltpu.make_async_copy(c_hbm.at[c], cbuf.at[own_s], local_sem.at[1]),
        pltpu.make_async_copy(first_hbm, first_in, local_sem.at[2]),
        pltpu.make_async_copy(second_hbm, second_in, local_sem.at[3]),
    ]
    for load in loads:
        load.start()
    pl.semaphore_wait(barrier, NB * NZ * NC - 1 + NB * NC + NY - 1)

    def pick_copy(m, k):
        return rdma(
            cand.at[m, :, pl.ds(pl.multiple_of((k % NZ) * LANES, LANES), LANES)],
            picked.at[d, c],
            pick_s.at[m, k],
            pick_r.at[d, c],
            k,
            a * (NY * NC) + y * NC + m,
        )

    def pick_self(m, k):
        return jnp.logical_and(c == m, k == d)

    for m in range(MATS):

        @pl.loop(0, NB * NZ)
        def _(k, m=m):
            @pl.when(jnp.logical_not(pick_self(m, k)))
            def _():
                pick_copy(m, k).start()

    lanes_own = pl.ds(pl.multiple_of(z * LANES, LANES), LANES)
    pick_own = pltpu.make_async_copy(cand.at[c, :, lanes_own], picked.at[d, c], pick_r.at[d, c])
    pick_own.start()

    def picks_left():
        for m in range(MATS):

            @pl.loop(0, NB * NZ)
            def _(k, m=m):
                @pl.when(jnp.logical_not(pick_self(m, k)))
                def _():
                    pick_copy(m, k).wait_send()

    leaving.append(picks_left)

    trio = ((0, 1), (1, 0), (1, 1))

    def trio_at(i):
        da, dc = trio[i]
        return (a + da) % NA, (c + dc) % NC

    def c_copy(i):
        oa, oc = trio_at(i)
        return rdma(c_hbm.at[oc], cbuf.at[own_s], c_s.at[i], c_r.at[own_s], d, oa * (NY * NC) + y * NC + oc)

    def x_copy(half, away):
        oa, oc = (1 - a, c) if away else (a, 1 - c)
        return rdma(
            x_hbm.at[half],
            xbuf.at[own_s, half],
            x_s.at[half, away],
            x_r.at[own_s, half],
            d,
            oa * (NY * NC) + y * NC + oc,
        )

    far_s = (1 - a) * NC + c

    def x_pass(half):
        return rdma(
            xbuf.at[far_s, half],
            xbuf.at[far_s, half],
            x_s.at[half, 2],
            x_r.at[far_s, half],
            d,
            a * (NY * NC) + y * NC + 1 - c,
        )

    for i in range(3):
        c_copy(i).start()
        leaving.append(c_copy(i).wait_send)
    for half in range(NA):
        x_copy(half, 1).start()
        leaving.append(x_copy(half, 1).wait_send)
    for half in range(NA):
        x_copy(half, 0).start()
        leaving.append(x_copy(half, 0).wait_send)

    for core in range(NC):

        @pl.loop(0, NB * NZ)
        def _(k, core=core):
            arrived(picked.at[k, core], pick_s.at[0, 0], pick_r.at[k, core])

    pt[y, :, :, lanes_own] = picked[owners[c]]
    order = (1, 7, 2, 6, 3, 5, 4)
    waves = range(2)

    def along_y(k):
        return d, a * (NY * NC) + ((y + k) % NY) * NC + c

    def along_z(k):
        return b * NZ + (z + k) % NZ, f

    def tile_copy(h, k):
        tile = pt.at[y, h, :, lanes_own]
        to = along_y(k) if h else along_z(k)
        return rdma(tile, tile, tile_s.at[h, k], tile_r.at[h, y if h else z], *to)

    def tile_arrived(h, k):
        source = ((y if h else z) + k) % NZ
        lanes = lanes_own if h else pl.ds(pl.multiple_of(source * LANES, LANES), LANES)
        arrived(pt.at[source if h else y, h, :, lanes], tile_s.at[0, 0], tile_r.at[h, source])

    def slab_copy(h, k):
        slab = pt.at[:, h, :, lanes_own] if h else pt.at[y, h]
        to = along_z(k) if h else along_y(k)
        return rdma(slab, slab, slab_s.at[h, k], slab_r.at[h, z if h else y], *to)

    def slab_arrived(h, k):
        source = ((z if h else y) + k) % NZ
        lanes = pl.ds(pl.multiple_of(source * LANES, LANES), LANES)
        arrived(pt.at[:, h, :, lanes] if h else pt.at[source, h], slab_s.at[0, 0], slab_r.at[h, source])

    for h in waves:
        for k in order:
            tile_copy(h, k).start()
            leaving.append(tile_copy(h, k).wait_send)
    for h in waves:
        for k in order:
            tile_arrived(h, k)
        for k in order:
            slab_copy(h, k).start()
            leaving.append(slab_copy(h, k).wait_send)

    tokens = NA * NC * cbuf.shape[1]

    def ring_slot(way, step):
        return (y - step + NY) % NY if way == 0 else (y + step) % NY

    def ring_copy(h, way, step):
        piece = ht.at[ring_slot(way, step - 1), h]
        to = along_y(1 if way == 0 else NY - 1)
        return rdma(piece, piece, h_s.at[h, way, step - 1], h_r.at[h, way, step - 1], *to)

    def ring_arrived(h, way, step):
        arrived(ht.at[ring_slot(way, step), h], h_s.at[0, 0, 0], h_r.at[h, way, step - 1])

    def forward(h, step):
        for way in range(2):
            if step > 1:
                ring_arrived(h, way, step - 1)
            if step < 4 or way == h:
                ring_copy(h, way, step).start()
                leaving.append(ring_copy(h, way, step).wait_send)

    def project(h):
        heads = lax.dot_general(
            pt[:, h].reshape(NY * 16, NZ * LANES),
            cbuf[...].reshape(tokens, NZ * LANES),
            (((1,), (1,)), ((), ())),
            preferred_element_type=jnp.float32,
        )
        ht[y, h] = heads.astype(jnp.bfloat16)

    def product(h, slots, blocks, start):
        left = jnp.concatenate([ht[slot, h] for slot in slots], axis=1)
        for s in blocks:
            right = jnp.concatenate([xbuf[s, :, slot].reshape(tokens, 256) for slot in slots], axis=0)
            part = jnp.dot(left, right, preferred_element_type=jnp.float32)
            acc[h, s] = part if start else acc[h, s] + part

    def rows_copy(i):
        oa, oc = trio_at(i)
        return rdma(
            pt.at[:, :, :, pl.ds(pl.multiple_of((d // 2) * LANES, LANES), LANES)],
            rows.at[c, a],
            rows_s.at[i],
            rows_r.at[own_s],
            d,
            oa * (NY * NC) + y * NC + oc,
        )

    def pass_on(half):
        arrived(xbuf.at[far_s, half], x_s.at[0, 0], x_r.at[far_s, half])
        x_pass(half).start()
        leaving.append(x_pass(half).wait_send)

    loads[1].wait()
    for i in range(3):
        oa, oc = trio_at(i)
        arrived(cbuf.at[oa * NC + oc], c_s.at[0], c_r.at[oa * NC + oc])
    for h in waves:
        for k in order:
            slab_arrived(h, k)
        project(h)
        forward(h, 1)
    for i in range(3):
        rows_copy(i).start()
        leaving.append(rows_copy(i).wait_send)
    rows[c, a] = pt[:, :, :, pl.ds(pl.multiple_of((d // 2) * LANES, LANES), LANES)]
    pass_on(0)
    forward(0, 2)
    forward(1, 2)
    forward(0, 3)
    pass_on(1)
    forward(1, 3)
    sib_s = a * NC + 1 - c
    other_s = (1 - a) * NC + 1 - c
    here, far = (own_s, sib_s), (far_s, other_s)
    near = (y, ring_slot(0, 1), ring_slot(1, 1))
    wide = (ring_slot(0, 2), ring_slot(1, 2), ring_slot(0, 3), ring_slot(1, 3))
    last = (ring_slot(0, 4),)
    loads[0].wait()
    for half in range(NA):
        arrived(xbuf.at[sib_s, half], x_s.at[0, 0], x_r.at[sib_s, half])
    product(0, near, here, True)
    forward(0, 4)
    product(1, near, here, True)
    forward(1, 4)
    for half in range(NA):
        arrived(xbuf.at[other_s, half], x_s.at[0, 0], x_r.at[other_s, half])

    def r_copy(h, k):
        to = (z + k) % NZ
        return rdma(rsend.at[h, to], rrecv.at[h, z], r_s.at[h, k], r_r.at[h, z], b * NZ + to, f)

    for h in waves:
        product(h, near, far, True)
        product(h, wide, here + far, False)
        ring_arrived(h, h, 4)
        product(h, last, here + far, False)
        for s in range(NA * NC):
            rsend[h, :, s] = acc[h, s].astype(jnp.bfloat16).reshape(NZ, 16, 256)
        for k in order:
            r_copy(h, k).start()
            leaving.append(r_copy(h, k).wait_send)

    for i in range(3):
        oa, oc = trio_at(i)
        arrived(rows.at[oc, oa], rows_s.at[0], rows_r.at[oa * NC + oc])
    for m in range(MATS):
        rows_t[m] = rows[m].reshape(512, LANES).T
    loads[2].wait()
    loads[3].wait()

    def f_self(s):
        return jnp.logical_and(s == own_s, a == b)

    def f_copy(h, s):
        return rdma(
            fsend.at[h, s],
            frecv.at[h, b, c],
            f_s.at[h, s],
            f_r.at[h, b * NC + c],
            a * NZ + z,
            (s // NC) * (NY * NC) + y * NC + s % NC,
        )

    def d_copy(h, k):
        to = along_z(k) if k else ((1 - b) * NZ + z, f)
        return rdma(dirs.at[d, h], dirs.at[d, h], d_s.at[h, k], d_r.at[h, d], *to)

    def d_pass(h, k):
        piece = dirs.at[b * NZ + (z + k) % NZ, h]
        return rdma(
            piece, piece, p_s.at[h, k], d_r.at[h, b * NZ + (z + k) % NZ], (1 - b) * NZ + z, f
        )

    inverse_root = 1.0 / math.sqrt(TOKENS)
    for h in waves:
        total = rsend[h, z].astype(jnp.float32)
        for k in order:
            source = (z + k) % NZ
            arrived(rrecv.at[h, source], r_s.at[0, 0], r_r.at[h, source])
            total = total + rrecv[h, source].astype(jnp.float32)
        fsend[h] = total.astype(jnp.bfloat16)
        for s in range(NA * NC):

            @pl.when(jnp.logical_not(f_self(s)))
            def _(h=h, s=s):
                f_copy(h, s).start()

            @pl.when(f_self(s))
            def _(h=h, s=s):
                pltpu.make_async_copy(fsend.at[h, s], frecv.at[h, b, c], f_r.at[h, b * NC + c]).start()

        for k in range(NB):
            for m in range(NC):
                arrived(frecv.at[h, k, m], f_s.at[0, 0], f_r.at[h, k * NC + m])
        block = slice(16 * h, 16 * h + 16)
        projected = (frecv[h, 0].astype(jnp.float32) + frecv[h, 1].astype(jnp.float32)) * inverse_root
        first = beta_first * first_in[:, block] + (1.0 - beta_first) * projected
        second = beta_second * second_in[:, block] + (1.0 - beta_second) * projected * projected
        direction = (
            first / (1.0 - beta_first**STEP) / (jnp.sqrt(second / (1.0 - beta_second**STEP)) + epsilon)
        )
        dirs[d, h] = direction.astype(jnp.bfloat16)
        for k in (0,) + order:
            d_copy(h, k).start()
            leaving.append(d_copy(h, k).wait_send)
        first_out[:, block] = first
        second_out[:, block] = second

    def f_left():
        for h in waves:
            for s in range(NA * NC):

                @pl.when(jnp.logical_not(f_self(s)))
                def _(h=h, s=s):
                    f_copy(h, s).wait_send()

    leaving.append(f_left)

    for h in waves:
        for k in order:
            source = b * NZ + (z + k) % NZ
            arrived(dirs.at[source, h], d_s.at[0, 0], d_r.at[h, source])
            d_pass(h, k).start()
            leaving.append(d_pass(h, k).wait_send)
    for h in waves:
        for k in (0,) + order:
            source = (1 - b) * NZ + (z + k) % NZ
            arrived(dirs.at[source, h], d_s.at[0, 0], d_r.at[h, source])

    for m in range(MATS):
        update_out[m] = jnp.dot(
            rows_t[m, pl.ds(pl.multiple_of((d % 2) * 64, 64), 64), :],
            dirs[:, :, m].reshape(512, 256),
            preferred_element_type=jnp.float32,
        ).astype(jnp.bfloat16)

    for wait in leaving:
        wait()


def on_device(layer_input, cotangent, candidates, moment_first, moment_second, owners):
    bf16, f32 = jnp.bfloat16, jnp.float32
    x = layer_input.reshape(NA, NY, 128, 256)
    cand = jnp.swapaxes(candidates[:, 0], 1, 2)
    vmem = pl.BlockSpec(memory_space=pltpu.VMEM)
    hbm = pl.BlockSpec(memory_space=pl.ANY)
    sem = pltpu.SemaphoreType.DMA
    return pl.pallas_call(
        kernel,
        out_shape=(
            jax.ShapeDtypeStruct((MATS, 64, 256), bf16),
            jax.ShapeDtypeStruct((MATS, 32, 256), f32),
            jax.ShapeDtypeStruct((MATS, 32, 256), f32),
        ),
        in_specs=[pl.BlockSpec(memory_space=pltpu.SMEM), hbm, hbm, hbm, hbm, hbm],
        out_specs=(vmem, vmem, vmem),
        scratch_shapes=[
            pltpu.VMEM((4, NA, NY, 128, 256), bf16),
            pltpu.VMEM((4, 64, 1024), bf16),
            pltpu.VMEM((16, NC, 16, LANES), bf16),
            pltpu.VMEM((NY, NB, 16, 1024), bf16),
            pltpu.VMEM((NY, 2, 128, 256), bf16),
            pltpu.VMEM((2, 4, 128, 256), f32),
            pltpu.VMEM((2, NZ, 4, 16, 256), bf16),
            pltpu.VMEM((2, NZ, 4, 16, 256), bf16),
            pltpu.VMEM((2, 4, 16, 256), bf16),
            pltpu.VMEM((2, NB, MATS, 16, 256), bf16),
            pltpu.VMEM((16, 2, MATS, 16, 256), bf16),
            pltpu.VMEM((MATS, NA, NY, NB, 16, LANES), bf16),
            pltpu.VMEM((MATS, LANES, 512), bf16),
            pltpu.VMEM((MATS, 32, 256), f32),
            pltpu.VMEM((MATS, 32, 256), f32),
            sem((4,)),
            sem((NA, 3)),
            sem((4, NA)),
            sem((3,)),
            sem((4,)),
            sem((MATS, 16)),
            sem((16, NC)),
            sem((2, NZ)),
            sem((2, NZ)),
            sem((2, NY)),
            sem((2, NY)),
            sem((3,)),
            sem((4,)),
            sem((2, 2, 4)),
            sem((2, 2, 4)),
            sem((2, NZ)),
            sem((2, NZ)),
            sem((2, 4)),
            sem((2, 4)),
            sem((2, NZ)),
            sem((2, 16)),
            sem((2, NZ)),
        ],
        compiler_params=pltpu.CompilerParams(
            collective_id=0, has_side_effects=True, vmem_limit_bytes=67043328
        ),
    )(owners, x, cotangent, cand, moment_first, moment_second)


def solution(mesh):
    placed = (
        P("dp", "fsdp"),
        P(None, ("dp", "fsdp"), None),
        P(None, "dp", None, "fsdp"),
        P(None, "dp", "fsdp"),
        P(None, "dp", "fsdp"),
        P(),
    )
    return jax.shard_map(
        on_device,
        mesh=mesh,
        in_specs=placed,
        out_specs=(P(None, "dp", "fsdp"), P(None, "dp", "fsdp"), P(None, "dp", "fsdp")),
        check_vma=False,
    )
```

time: 95.9 us -> 86 us (0.90)
  Pallas kernels: 91.5 us -> 81.8 us
    pallas_call x1, Pallas kernels: 91.5 us -> 81.8 us  [on_device(): pl.pallas_call(kernel, out_shape=(jax.ShapeDtypeStruct((MATS, 64, 256), b...]
where the time goes in v3:
time: 86 us; the launch traced here: 85.4 us
  Pallas kernels  81.8 us (95%)
  local copies, waits for them, and re-layouts  3 us (3%)
    pallas_call x1, Pallas kernels, on_device(): pl.pallas_call(kernel, out_shape=(jax.ShapeDtypeStruct((MATS, 64, 256), b...  81.8 us
    unnamed x7, local copies, waits for them, and re-layouts  3 us

profile of v3, /device:TPU:1, one launch (start us, length us, event | category | flops | bytes accessed | tf_op | source)
XLA Modules:
  0.0 85.4 jit_solution(18271327940445498454)
XLA Ops:
  0.6 81.8 %shard_map.85 = (bf16[2,64,256]{2,1,0:T(8,128)(2,1)}, f32[2,32,256]{2,1,0:T(8,128)}, f32[2,32,256]{2,1,0:T(8,128)}) custom-call(s32[2]{0:T(128)} %owners.1, bf16[2,8,128,256]{3,2,1,0:T(8,128)(2,1)} %bitcast.4, bf16[2,64,1024]{2,1,0:T(8,128)(2,1)} %c_hbm.1, bf16[2,16,1024]{2,1,0:T(8,128)(2,1)} %bitcast.5, f32[2,32,256]{2,1,0:T(8,128)} %first_hbm.1, ...), custom_call_target="tpu_custom_call" | custom-call | tf_op jit(solution)/shard_map/pallas_call | solution.py:456
  82.4 0.0 copy-start.1
  82.4 1.5 %copy.12 = bf16[2,64,256]{2,1,0:T(8,128)(2,1)} copy(bf16[2,64,256]{2,1,0:T(8,128)(2,1)} %get-tuple-element.6) | data formatting | bytes 131072
  83.9 0.0 copy-done.1
  83.9 0.0 copy-start
  83.9 0.6 copy.13
  84.6 0.2 copy-done
  84.8 0.6 copy.14
Async XLA Ops:
  82.4 1.5 %copy-start.1 = (f32[2,32,256]{2,1,0:T(8,128)S(1)}, f32[2,32,256]{2,1,0:T(8,128)}, u32[]{:S(2)}) copy-start(f32[2,32,256]{2,1,0:T(8,128)} %get-tuple-element.7) | copy-start | bytes 196612
  83.9 0.9 %copy-start = (f32[2,32,256]{2,1,0:T(8,128)S(1)}, f32[2,32,256]{2,1,0:T(8,128)}, u32[]{:S(2)}) copy-start(f32[2,32,256]{2,1,0:T(8,128)} %get-tuple-element.8) | copy-start | bytes 196612

commit v4 on v3

--- a/solution.py
+++ b/solution.py
@@ -32,18 +32,18 @@
     first_hbm,
     second_hbm,
     update_out,
-    first_out,
-    second_out,
+    projected_out,
     xbuf,
     cbuf,
+    cbuf_t,
     picked,
     pt,
     ht,
     acc,
+    bsend,
+    brecv,
     rsend,
     rrecv,
-    fsend,
-    frecv,
     dirs,
     rows,
     rows_t,
@@ -64,10 +64,10 @@
     rows_r,
     h_s,
     h_r,
+    b_s,
+    b_r,
     r_s,
     r_r,
-    f_s,
-    f_r,
     d_s,
     d_r,
     p_s,
@@ -205,7 +205,7 @@
             arrived(picked.at[k, core], pick_s.at[0, 0], pick_r.at[k, core])
 
     pt[y, :, :, lanes_own] = picked[owners[c]]
-    order = (1, 7, 2, 6, 3, 5, 4)
+    order = (4, 3, 5, 2, 6, 1, 7)
     waves = range(2)
 
     def along_y(k):
@@ -269,8 +269,8 @@
     def project(h):
         heads = lax.dot_general(
             pt[:, h].reshape(NY * 16, NZ * LANES),
-            cbuf[...].reshape(tokens, NZ * LANES),
-            (((1,), (1,)), ((), ())),
+            cbuf_t[...],
+            (((1,), (0,)), ((), ())),
             preferred_element_type=jnp.float32,
         )
         ht[y, h] = heads.astype(jnp.bfloat16)
@@ -302,6 +302,7 @@
     for i in range(3):
         oa, oc = trio_at(i)
         arrived(cbuf.at[oa * NC + oc], c_s.at[0], c_r.at[oa * NC + oc])
+    cbuf_t[...] = cbuf[...].reshape(tokens, NZ * LANES).T
     for h in waves:
         for k in order:
             slab_arrived(h, k)
@@ -315,8 +316,8 @@
     forward(0, 2)
     forward(1, 2)
     forward(0, 3)
+    forward(1, 3)
     pass_on(1)
-    forward(1, 3)
     sib_s = a * NC + 1 - c
     other_s = (1 - a) * NC + 1 - c
     here, far = (own_s, sib_s), (far_s, other_s)
@@ -333,41 +334,77 @@
     for half in range(NA):
         arrived(xbuf.at[other_s, half], x_s.at[0, 0], x_r.at[other_s, half])
 
-    def r_copy(h, k):
+    def b_copy(h, k):
         to = (z + k) % NZ
-        return rdma(rsend.at[h, to], rrecv.at[h, z], r_s.at[h, k], r_r.at[h, z], b * NZ + to, f)
+        return rdma(
+            bsend.at[h, to], brecv.at[h, to], b_s.at[h, k], b_r.at[h, to], (1 - b) * NZ + z, f
+        )
+
+    def r_copy(h, k, core):
+        to = (z + k) % NZ
+        return rdma(
+            rsend.at[h, to, core],
+            rrecv.at[h, c, z],
+            r_s.at[h, k, core],
+            r_r.at[h, c, z],
+            a * NZ + to,
+            b * (NY * NC) + y * NC + core,
+        )
+
+    def r_self(core):
+        return jnp.logical_and(core == c, a == b)
 
     for h in waves:
         product(h, near, far, True)
         product(h, wide, here + far, False)
+    for h in waves:
         ring_arrived(h, h, 4)
         product(h, last, here + far, False)
-        for s in range(NA * NC):
-            rsend[h, :, s] = acc[h, s].astype(jnp.bfloat16).reshape(NZ, 16, 256)
-        for k in order:
-            r_copy(h, k).start()
-            leaving.append(r_copy(h, k).wait_send)
-
+        for core in range(NC):
+            bsend[h, :, core] = acc[h, (1 - b) * NC + core].astype(jnp.bfloat16).reshape(NZ, 16, 256)
+        for k in order + (0,):
+            b_copy(h, k).start()
+            leaving.append(b_copy(h, k).wait_send)
+
+    def both(h, to):
+        arrived(brecv.at[h, to], b_s.at[0, 0], b_r.at[h, to])
+        mine = [acc[h, b * NC + core, pl.ds(pl.multiple_of(to * 16, 16), 16), :] for core in range(NC)]
+        return jnp.stack(mine) + brecv[h, to].astype(jnp.float32)
+
+    for h in waves:
+        for k in order + (0,):
+            rsend[h, (z + k) % NZ] = both(h, (z + k) % NZ).astype(jnp.bfloat16)
+            for core in range(NC):
+                if k:
+                    r_copy(h, k, core).start()
+                    leaving.append(r_copy(h, k, core).wait_send)
+                else:
+
+                    @pl.when(jnp.logical_not(r_self(core)))
+                    def _(h=h, core=core):
+                        r_copy(h, 0, core).start()
+
+                    @pl.when(r_self(core))
+                    def _(h=h, core=core):
+                        pltpu.make_async_copy(rsend.at[h, z, core], rrecv.at[h, c, z], r_r.at[h, c, z]).start()
+
+    def r_left():
+        for h in waves:
+            for core in range(NC):
+
+                @pl.when(jnp.logical_not(r_self(core)))
+                def _(h=h, core=core):
+                    r_copy(h, 0, core).wait_send()
+
+    leaving.append(r_left)
     for i in range(3):
         oa, oc = trio_at(i)
         arrived(rows.at[oc, oa], rows_s.at[0], rows_r.at[oa * NC + oc])
     for m in range(MATS):
-        rows_t[m] = rows[m].reshape(512, LANES).T
+        for h in waves:
+            rows_t[m, h] = rows[m, :, :, h].reshape(256, LANES).T
     loads[2].wait()
     loads[3].wait()
-
-    def f_self(s):
-        return jnp.logical_and(s == own_s, a == b)
-
-    def f_copy(h, s):
-        return rdma(
-            fsend.at[h, s],
-            frecv.at[h, b, c],
-            f_s.at[h, s],
-            f_r.at[h, b * NC + c],
-            a * NZ + z,
-            (s // NC) * (NY * NC) + y * NC + s % NC,
-        )
 
     def d_copy(h, k):
         to = along_z(k) if k else ((1 - b) * NZ + z, f)
@@ -381,27 +418,11 @@
 
     inverse_root = 1.0 / math.sqrt(TOKENS)
     for h in waves:
-        total = rsend[h, z].astype(jnp.float32)
-        for k in order:
-            source = (z + k) % NZ
-            arrived(rrecv.at[h, source], r_s.at[0, 0], r_r.at[h, source])
-            total = total + rrecv[h, source].astype(jnp.float32)
-        fsend[h] = total.astype(jnp.bfloat16)
-        for s in range(NA * NC):
-
-            @pl.when(jnp.logical_not(f_self(s)))
-            def _(h=h, s=s):
-                f_copy(h, s).start()
-
-            @pl.when(f_self(s))
-            def _(h=h, s=s):
-                pltpu.make_async_copy(fsend.at[h, s], frecv.at[h, b, c], f_r.at[h, b * NC + c]).start()
-
-        for k in range(NB):
-            for m in range(NC):
-                arrived(frecv.at[h, k, m], f_s.at[0, 0], f_r.at[h, k * NC + m])
+        for k in (0,) + order:
+            for m in range(MATS):
+                arrived(rrecv.at[h, m, (z + k) % NZ], r_s.at[0, 0, 0], r_r.at[h, m, (z + k) % NZ])
         block = slice(16 * h, 16 * h + 16)
-        projected = (frecv[h, 0].astype(jnp.float32) + frecv[h, 1].astype(jnp.float32)) * inverse_root
+        projected = jnp.sum(rrecv[h].astype(jnp.float32), axis=1) * inverse_root
         first = beta_first * first_in[:, block] + (1.0 - beta_first) * projected
         second = beta_second * second_in[:, block] + (1.0 - beta_second) * projected * projected
         direction = (
@@ -411,18 +432,7 @@
         for k in (0,) + order:
             d_copy(h, k).start()
             leaving.append(d_copy(h, k).wait_send)
-        first_out[:, block] = first
-        second_out[:, block] = second
-
-    def f_left():
-        for h in waves:
-            for s in range(NA * NC):
-
-                @pl.when(jnp.logical_not(f_self(s)))
-                def _(h=h, s=s):
-                    f_copy(h, s).wait_send()
-
-    leaving.append(f_left)
+        projected_out[:, block] = projected
 
     for h in waves:
         for k in order:
@@ -430,17 +440,24 @@
             arrived(dirs.at[source, h], d_s.at[0, 0], d_r.at[h, source])
             d_pass(h, k).start()
             leaving.append(d_pass(h, k).wait_send)
+    updates = []
+    own_rows = pl.ds(pl.multiple_of((d % 2) * 64, 64), 64)
     for h in waves:
         for k in (0,) + order:
             source = (1 - b) * NZ + (z + k) % NZ
             arrived(dirs.at[source, h], d_s.at[0, 0], d_r.at[h, source])
-
+        updates.append(
+            [
+                jnp.dot(
+                    rows_t[m, h, own_rows, :],
+                    dirs[:, h, m].reshape(256, 256),
+                    preferred_element_type=jnp.float32,
+                )
+                for m in range(MATS)
+            ]
+        )
     for m in range(MATS):
-        update_out[m] = jnp.dot(
-            rows_t[m, pl.ds(pl.multiple_of((d % 2) * 64, 64), 64), :],
-            dirs[:, :, m].reshape(512, 256),
-            preferred_element_type=jnp.float32,
-        ).astype(jnp.bfloat16)
+        update_out[m] = updates[0][m] + updates[1][m]
 
     for wait in leaving:
         wait()
@@ -453,29 +470,29 @@
     vmem = pl.BlockSpec(memory_space=pltpu.VMEM)
     hbm = pl.BlockSpec(memory_space=pl.ANY)
     sem = pltpu.SemaphoreType.DMA
-    return pl.pallas_call(
+    update, projected = pl.pallas_call(
         kernel,
         out_shape=(
-            jax.ShapeDtypeStruct((MATS, 64, 256), bf16),
-            jax.ShapeDtypeStruct((MATS, 32, 256), f32),
+            jax.ShapeDtypeStruct((MATS, 64, 256), f32),
             jax.ShapeDtypeStruct((MATS, 32, 256), f32),
         ),
         in_specs=[pl.BlockSpec(memory_space=pltpu.SMEM), hbm, hbm, hbm, hbm, hbm],
-        out_specs=(vmem, vmem, vmem),
+        out_specs=(vmem, vmem),
         scratch_shapes=[
             pltpu.VMEM((4, NA, NY, 128, 256), bf16),
             pltpu.VMEM((4, 64, 1024), bf16),
+            pltpu.VMEM((1024, 256), bf16),
             pltpu.VMEM((16, NC, 16, LANES), bf16),
             pltpu.VMEM((NY, NB, 16, 1024), bf16),
             pltpu.VMEM((NY, 2, 128, 256), bf16),
             pltpu.VMEM((2, 4, 128, 256), f32),
-            pltpu.VMEM((2, NZ, 4, 16, 256), bf16),
-            pltpu.VMEM((2, NZ, 4, 16, 256), bf16),
-            pltpu.VMEM((2, 4, 16, 256), bf16),
-            pltpu.VMEM((2, NB, MATS, 16, 256), bf16),
+            pltpu.VMEM((2, NZ, NC, 16, 256), bf16),
+            pltpu.VMEM((2, NZ, NC, 16, 256), bf16),
+            pltpu.VMEM((2, NZ, NC, 16, 256), bf16),
+            pltpu.VMEM((2, MATS, NZ, 16, 256), bf16),
             pltpu.VMEM((16, 2, MATS, 16, 256), bf16),
             pltpu.VMEM((MATS, NA, NY, NB, 16, LANES), bf16),
-            pltpu.VMEM((MATS, LANES, 512), bf16),
+            pltpu.VMEM((MATS, 2, LANES, 256), bf16),
             pltpu.VMEM((MATS, 32, 256), f32),
             pltpu.VMEM((MATS, 32, 256), f32),
             sem((4,)),
@@ -495,8 +512,8 @@
             sem((2, 2, 4)),
             sem((2, NZ)),
             sem((2, NZ)),
-            sem((2, 4)),
-            sem((2, 4)),
+            sem((2, NZ, NC)),
+            sem((2, MATS, NZ)),
             sem((2, NZ)),
             sem((2, 16)),
             sem((2, NZ)),
@@ -505,6 +522,9 @@
             collective_id=0, has_side_effects=True, vmem_limit_bytes=67043328
         ),
     )(owners, x, cotangent, cand, moment_first, moment_second)
+    first = beta_first * moment_first + (1.0 - beta_first) * projected
+    second = beta_second * moment_second + (1.0 - beta_second) * projected * projected
+    return update.astype(bf16), first, second
 
 
 def solution(mesh):

time: 86 us -> 80.7 us (0.938)
  Pallas kernels: 81.8 us -> 77.5 us
  local copies, waits for them, and re-layouts: 3 us -> 0.02 us
  other arithmetic: 0 us -> 2.26 us
    pallas_call x1, Pallas kernels: 81.8 us -> 77.5 us  [on_device(): pl.pallas_call(kernel, out_shape=(jax.ShapeDtypeStruct((MATS, 64, 256), f...]
    unnamed x7 -> x6, local copies, waits for them, and re-layouts: 3 us -> 0.02 us
    convert_element_type x0 -> x1, other arithmetic: none -> 1.59 us  [on_device(): return (update.astype(bf16), first, second)]
where the time goes in v4:
time: 80.7 us; the launch traced here: 80.5 us
  Pallas kernels  77.5 us (96%)
  other arithmetic  2.26 us (3%)
    pallas_call x1, Pallas kernels, on_device(): pl.pallas_call(kernel, out_shape=(jax.ShapeDtypeStruct((MATS, 64, 256), f...  77.5 us

profile of v4, /device:TPU:1, one launch (start us, length us, event | category | flops | bytes accessed | tf_op | source)
XLA Modules:
  0.0 80.5 jit_solution(1951230242023229811)
XLA Ops:
  0.6 77.5 %shard_map.85 = (f32[2,64,256]{2,1,0:T(8,128)}, f32[2,32,256]{2,1,0:T(8,128)}) custom-call(s32[2]{0:T(128)} %owners.1, bf16[2,8,128,256]{3,2,1,0:T(8,128)(2,1)} %bitcast.4, bf16[2,64,1024]{2,1,0:T(8,128)(2,1)} %c_hbm.1, bf16[2,16,1024]{2,1,0:T(8,128)(2,1)} %bitcast.5, f32[2,32,256]{2,1,0:T(8,128)} %first_hbm.1, f32[2,32,256]{2,1,0:T(8,128)} %second_hbm.1), custom_call_target="tpu_custom_call" | custom-call | tf_op jit(solution)/shard_map/pallas_call | solution.py:473
  78.2 0.0 copy-start
  78.2 0.0 copy-start.1
  78.2 0.0 copy-start.2
  78.2 1.6 %convert_element_type.3 = bf16[2,64,256]{2,1,0:T(8,128)(2,1)} convert(f32[2,64,256]{2,1,0:T(8,128)} %get-tuple-element.5) | non-fusion elementwise | flops 32768 | bytes 196608 | tf_op jit(solution)/shard_map/convert_element_type | solution.py:527
  79.8 0.0 copy-done
  79.8 0.0 copy-done.1
  79.8 0.0 copy-done.2
  79.8 0.7 fusion
Async XLA Ops:
  78.2 1.6 %copy-start = (f32[2,32,256]{2,1,0:T(8,128)S(1)}, f32[2,32,256]{2,1,0:T(8,128)}, u32[]{:S(2)}) copy-start(f32[2,32,256]{2,1,0:T(8,128)} %first_hbm.1) | copy-start | bytes 196612
  78.2 1.6 %copy-start.1 = (f32[2,32,256]{2,1,0:T(8,128)S(1)}, f32[2,32,256]{2,1,0:T(8,128)}, u32[]{:S(2)}) copy-start(f32[2,32,256]{2,1,0:T(8,128)} %second_hbm.1) | copy-start | bytes 196612
  78.2 1.6 %copy-start.2 = (f32[2,32,256]{2,1,0:T(8,128)S(1)}, f32[2,32,256]{2,1,0:T(8,128)}, u32[]{:S(2)}) copy-start(f32[2,32,256]{2,1,0:T(8,128)} %get-tuple-element.6) | copy-start | bytes 196612

commit v5 on v4

--- a/solution.py
+++ b/solution.py
@@ -25,7 +25,7 @@
 
 
 def kernel(
-    owners,
+    owners_hbm,
     x_hbm,
     c_hbm,
     cand,
@@ -38,6 +38,7 @@
     cbuf_t,
     picked,
     pt,
+    qt,
     ht,
     acc,
     bsend,
@@ -49,6 +50,7 @@
     rows_t,
     first_in,
     second_in,
+    owners,
     local_sem,
     x_s,
     x_r,
@@ -109,6 +111,8 @@
     for k in range(1, NY):
         greet(d, a * (NY * NC) + ((y + k) % NY) * NC + c)
 
+    owners_load = pltpu.make_async_copy(owners_hbm, owners, local_sem.at[4])
+    owners_load.start()
     loads = [
         pltpu.make_async_copy(x_hbm, xbuf.at[own_s], local_sem.at[0]),
         pltpu.make_async_copy(c_hbm.at[c], cbuf.at[own_s], local_sem.at[1]),
@@ -165,11 +169,16 @@
         oa, oc = trio_at(i)
         return rdma(c_hbm.at[oc], cbuf.at[own_s], c_s.at[i], c_r.at[own_s], d, oa * (NY * NC) + y * NC + oc)
 
+    parts = range(4)
+
+    def x_part(ref, part):
+        return ref.at[part // 2, pl.ds(part % 2 * 4, 4)]
+
     def x_copy(half, away):
         oa, oc = (1 - a, c) if away else (a, 1 - c)
         return rdma(
-            x_hbm.at[half],
-            xbuf.at[own_s, half],
+            x_part(x_hbm, half),
+            x_part(xbuf.at[own_s], half),
             x_s.at[half, away],
             x_r.at[own_s, half],
             d,
@@ -180,8 +189,8 @@
 
     def x_pass(half):
         return rdma(
-            xbuf.at[far_s, half],
-            xbuf.at[far_s, half],
+            x_part(xbuf.at[far_s], half),
+            x_part(xbuf.at[far_s], half),
             x_s.at[half, 2],
             x_r.at[far_s, half],
             d,
@@ -191,10 +200,10 @@
     for i in range(3):
         c_copy(i).start()
         leaving.append(c_copy(i).wait_send)
-    for half in range(NA):
+    for half in parts:
         x_copy(half, 1).start()
         leaving.append(x_copy(half, 1).wait_send)
-    for half in range(NA):
+    for half in parts:
         x_copy(half, 0).start()
         leaving.append(x_copy(half, 0).wait_send)
 
@@ -204,7 +213,10 @@
         def _(k, core=core):
             arrived(picked.at[k, core], pick_s.at[0, 0], pick_r.at[k, core])
 
-    pt[y, :, :, lanes_own] = picked[owners[c]]
+    owners_load.wait()
+    chosen = picked[owners[c]]
+    pt[y, :, lanes_own] = chosen[0]
+    qt[z, y] = chosen[1]
     order = (4, 3, 5, 2, 6, 1, 7)
     waves = range(2)
 
@@ -214,38 +226,45 @@
     def along_z(k):
         return b * NZ + (z + k) % NZ, f
 
+    def lanes_of(k):
+        return pl.ds(pl.multiple_of((z + k) % NZ * LANES, LANES), LANES)
+
+    def tile_of(h, k):
+        return qt.at[z, (y + k) % NY] if h else pt.at[y, :, lanes_of(k)]
+
     def tile_copy(h, k):
-        tile = pt.at[y, h, :, lanes_own]
         to = along_y(k) if h else along_z(k)
-        return rdma(tile, tile, tile_s.at[h, k], tile_r.at[h, y if h else z], *to)
+        return rdma(tile_of(h, 0), tile_of(h, 0), tile_s.at[h, k], tile_r.at[h, y if h else z], *to)
 
     def tile_arrived(h, k):
-        source = ((y if h else z) + k) % NZ
-        lanes = lanes_own if h else pl.ds(pl.multiple_of(source * LANES, LANES), LANES)
-        arrived(pt.at[source if h else y, h, :, lanes], tile_s.at[0, 0], tile_r.at[h, source])
+        arrived(tile_of(h, k), tile_s.at[0, 0], tile_r.at[h, ((y if h else z) + k) % NZ])
+
+    def slab_of(h, k):
+        return qt.at[(z + k) % NZ] if h else pt.at[(y + k) % NY]
 
     def slab_copy(h, k):
-        slab = pt.at[:, h, :, lanes_own] if h else pt.at[y, h]
         to = along_z(k) if h else along_y(k)
-        return rdma(slab, slab, slab_s.at[h, k], slab_r.at[h, z if h else y], *to)
+        return rdma(slab_of(h, 0), slab_of(h, 0), slab_s.at[h, k], slab_r.at[h, z if h else y], *to)
 
     def slab_arrived(h, k):
-        source = ((z if h else y) + k) % NZ
-        lanes = pl.ds(pl.multiple_of(source * LANES, LANES), LANES)
-        arrived(pt.at[:, h, :, lanes] if h else pt.at[source, h], slab_s.at[0, 0], slab_r.at[h, source])
+        arrived(slab_of(h, k), slab_s.at[0, 0], slab_r.at[h, ((z if h else y) + k) % NZ])
 
     for h in waves:
         for k in order:
             tile_copy(h, k).start()
             leaving.append(tile_copy(h, k).wait_send)
+    tokens = NA * NC * cbuf.shape[1]
+    loads[1].wait()
+    for i in range(3):
+        oa, oc = trio_at(i)
+        arrived(cbuf.at[oa * NC + oc], c_s.at[0], c_r.at[oa * NC + oc])
+    cbuf_t[...] = cbuf[...].reshape(tokens, NZ * LANES).T
     for h in waves:
         for k in order:
             tile_arrived(h, k)
         for k in order:
             slab_copy(h, k).start()
             leaving.append(slab_copy(h, k).wait_send)
-
-    tokens = NA * NC * cbuf.shape[1]
 
     def ring_slot(way, step):
         return (y - step + NY) % NY if way == 0 else (y + step) % NY
@@ -267,12 +286,11 @@
                 leaving.append(ring_copy(h, way, step).wait_send)
 
     def project(h):
-        heads = lax.dot_general(
-            pt[:, h].reshape(NY * 16, NZ * LANES),
-            cbuf_t[...],
-            (((1,), (0,)), ((), ())),
-            preferred_element_type=jnp.float32,
-        )
+        if h == 0:
+            left = pt[...].reshape(NY * 16, NZ * LANES)
+        else:
+            left = jnp.concatenate([qt[k].reshape(NY * 16, LANES) for k in range(NZ)], axis=1)
+        heads = jnp.dot(left, cbuf_t[...], preferred_element_type=jnp.float32)
         ht[y, h] = heads.astype(jnp.bfloat16)
 
     def product(h, slots, blocks, start):
@@ -282,42 +300,44 @@
             part = jnp.dot(left, right, preferred_element_type=jnp.float32)
             acc[h, s] = part if start else acc[h, s] + part
 
-    def rows_copy(i):
+    def rows_of(h):
+        block = d // 2
+        return qt.at[block] if h else pt.at[:, :, pl.ds(pl.multiple_of(block * LANES, LANES), LANES)]
+
+    def rows_copy(h, i):
         oa, oc = trio_at(i)
         return rdma(
-            pt.at[:, :, :, pl.ds(pl.multiple_of((d // 2) * LANES, LANES), LANES)],
-            rows.at[c, a],
-            rows_s.at[i],
-            rows_r.at[own_s],
+            rows_of(h),
+            rows.at[c, a, h],
+            rows_s.at[h, i],
+            rows_r.at[h, own_s],
             d,
             oa * (NY * NC) + y * NC + oc,
         )
 
     def pass_on(half):
-        arrived(xbuf.at[far_s, half], x_s.at[0, 0], x_r.at[far_s, half])
+        arrived(x_part(xbuf.at[far_s], half), x_s.at[0, 0], x_r.at[far_s, half])
         x_pass(half).start()
         leaving.append(x_pass(half).wait_send)
 
-    loads[1].wait()
-    for i in range(3):
-        oa, oc = trio_at(i)
-        arrived(cbuf.at[oa * NC + oc], c_s.at[0], c_r.at[oa * NC + oc])
-    cbuf_t[...] = cbuf[...].reshape(tokens, NZ * LANES).T
     for h in waves:
         for k in order:
             slab_arrived(h, k)
         project(h)
         forward(h, 1)
-    for i in range(3):
-        rows_copy(i).start()
-        leaving.append(rows_copy(i).wait_send)
-    rows[c, a] = pt[:, :, :, pl.ds(pl.multiple_of((d // 2) * LANES, LANES), LANES)]
+    for h in waves:
+        for i in range(3):
+            rows_copy(h, i).start()
+            leaving.append(rows_copy(h, i).wait_send)
+        rows[c, a, h] = rows_of(h)[...]
     pass_on(0)
+    pass_on(1)
     forward(0, 2)
     forward(1, 2)
     forward(0, 3)
     forward(1, 3)
-    pass_on(1)
+    pass_on(2)
+    pass_on(3)
     sib_s = a * NC + 1 - c
     other_s = (1 - a) * NC + 1 - c
     here, far = (own_s, sib_s), (far_s, other_s)
@@ -325,14 +345,14 @@
     wide = (ring_slot(0, 2), ring_slot(1, 2), ring_slot(0, 3), ring_slot(1, 3))
     last = (ring_slot(0, 4),)
     loads[0].wait()
-    for half in range(NA):
-        arrived(xbuf.at[sib_s, half], x_s.at[0, 0], x_r.at[sib_s, half])
+    for half in parts:
+        arrived(x_part(xbuf.at[sib_s], half), x_s.at[0, 0], x_r.at[sib_s, half])
     product(0, near, here, True)
     forward(0, 4)
     product(1, near, here, True)
     forward(1, 4)
-    for half in range(NA):
-        arrived(xbuf.at[other_s, half], x_s.at[0, 0], x_r.at[other_s, half])
+    for half in parts:
+        arrived(x_part(xbuf.at[other_s], half), x_s.at[0, 0], x_r.at[other_s, half])
 
     def b_copy(h, k):
         to = (z + k) % NZ
@@ -399,10 +419,11 @@
     leaving.append(r_left)
     for i in range(3):
         oa, oc = trio_at(i)
-        arrived(rows.at[oc, oa], rows_s.at[0], rows_r.at[oa * NC + oc])
+        for h in waves:
+            arrived(rows.at[oc, oa, h], rows_s.at[0, 0], rows_r.at[h, oa * NC + oc])
     for m in range(MATS):
         for h in waves:
-            rows_t[m, h] = rows[m, :, :, h].reshape(256, LANES).T
+            rows_t[m, h] = rows[m, :, h].reshape(256, LANES).T
     loads[2].wait()
     loads[3].wait()
 
@@ -434,6 +455,9 @@
             leaving.append(d_copy(h, k).wait_send)
         projected_out[:, block] = projected
 
+    for wait in leaving[: len(leaving) - 2 * NZ]:
+        wait()
+    del leaving[: len(leaving) - 2 * NZ]
     for h in waves:
         for k in order:
             source = b * NZ + (z + k) % NZ
@@ -476,14 +500,15 @@
             jax.ShapeDtypeStruct((MATS, 64, 256), f32),
             jax.ShapeDtypeStruct((MATS, 32, 256), f32),
         ),
-        in_specs=[pl.BlockSpec(memory_space=pltpu.SMEM), hbm, hbm, hbm, hbm, hbm],
+        in_specs=[hbm] * 6,
         out_specs=(vmem, vmem),
         scratch_shapes=[
             pltpu.VMEM((4, NA, NY, 128, 256), bf16),
             pltpu.VMEM((4, 64, 1024), bf16),
             pltpu.VMEM((1024, 256), bf16),
             pltpu.VMEM((16, NC, 16, LANES), bf16),
-            pltpu.VMEM((NY, NB, 16, 1024), bf16),
+            pltpu.VMEM((NY, 16, 1024), bf16),
+            pltpu.VMEM((NZ, NY, 16, LANES), bf16),
             pltpu.VMEM((NY, 2, 128, 256), bf16),
             pltpu.VMEM((2, 4, 128, 256), f32),
             pltpu.VMEM((2, NZ, NC, 16, 256), bf16),
@@ -491,13 +516,14 @@
             pltpu.VMEM((2, NZ, NC, 16, 256), bf16),
             pltpu.VMEM((2, MATS, NZ, 16, 256), bf16),
             pltpu.VMEM((16, 2, MATS, 16, 256), bf16),
-            pltpu.VMEM((MATS, NA, NY, NB, 16, LANES), bf16),
+            pltpu.VMEM((MATS, NA, 2, NY, 16, LANES), bf16),
             pltpu.VMEM((MATS, 2, LANES, 256), bf16),
             pltpu.VMEM((MATS, 32, 256), f32),
             pltpu.VMEM((MATS, 32, 256), f32),
-            sem((4,)),
-            sem((NA, 3)),
-            sem((4, NA)),
+            pltpu.SMEM((MATS,), jnp.int32),
+            sem((5,)),
+            sem((4, 3)),
+            sem((4, 4)),
             sem((3,)),
             sem((4,)),
             sem((MATS, 16)),
@@ -506,8 +532,8 @@
             sem((2, NZ)),
             sem((2, NY)),
             sem((2, NY)),
-            sem((3,)),
-            sem((4,)),
+            sem((2, 3)),
+            sem((2, 4)),
             sem((2, 2, 4)),
             sem((2, 2, 4)),
             sem((2, NZ)),

time: 80.7 us -> 79.4 us (0.984)
  Pallas kernels: 77.5 us -> 76.3 us
    pallas_call x1, Pallas kernels: 77.5 us -> 76.3 us  [on_device(): pl.pallas_call(kernel, out_shape=(jax.ShapeDtypeStruct((MATS, 64, 256), f...]
where the time goes in v5:
time: 79.4 us; the launch traced here: 79.2 us
  Pallas kernels  76.3 us (96%)
  other arithmetic  2.26 us (3%)
    pallas_call x1, Pallas kernels, on_device(): pl.pallas_call(kernel, out_shape=(jax.ShapeDtypeStruct((MATS, 64, 256), f...  76.3 us

profile of v5, /device:TPU:1, one launch (start us, length us, event | category | flops | bytes accessed | tf_op | source)
XLA Modules:
  0.0 79.2 jit_solution(12054616799802462389)
XLA Ops:
  0.6 76.3 %shard_map.85 = (f32[2,64,256]{2,1,0:T(8,128)}, f32[2,32,256]{2,1,0:T(8,128)}) custom-call(s32[2]{0:T(128)} %owners_hbm.1, bf16[2,8,128,256]{3,2,1,0:T(8,128)(2,1)} %bitcast.4, bf16[2,64,1024]{2,1,0:T(8,128)(2,1)} %c_hbm.1, bf16[2,16,1024]{2,1,0:T(8,128)(2,1)} %bitcast.5, f32[2,32,256]{2,1,0:T(8,128)} %first_hbm.1, f32[2,32,256]{2,1,0:T(8,128)} %second_hbm.1), custom_call_target="tpu_custom_call" | custom-call | tf_op jit(solution)/shard_map/pallas_call | solution.py:497
  76.9 0.0 copy-start
  76.9 0.0 copy-start.1
  76.9 0.0 copy-start.2
  77.0 1.6 %convert_element_type.3 = bf16[2,64,256]{2,1,0:T(8,128)(2,1)} convert(f32[2,64,256]{2,1,0:T(8,128)} %get-tuple-element.5) | non-fusion elementwise | flops 32768 | bytes 196608 | tf_op jit(solution)/shard_map/convert_element_type | solution.py:553
  78.5 0.0 copy-done
  78.5 0.0 copy-done.1
  78.6 0.0 copy-done.2
  78.6 0.7 fusion
Async XLA Ops:
  76.9 1.6 %copy-start = (f32[2,32,256]{2,1,0:T(8,128)S(1)}, f32[2,32,256]{2,1,0:T(8,128)}, u32[]{:S(2)}) copy-start(f32[2,32,256]{2,1,0:T(8,128)} %first_hbm.1) | copy-start | bytes 196612
  76.9 1.6 %copy-start.1 = (f32[2,32,256]{2,1,0:T(8,128)S(1)}, f32[2,32,256]{2,1,0:T(8,128)}, u32[]{:S(2)}) copy-start(f32[2,32,256]{2,1,0:T(8,128)} %second_hbm.1) | copy-start | bytes 196612
  76.9 1.6 %copy-start.2 = (f32[2,32,256]{2,1,0:T(8,128)S(1)}, f32[2,32,256]{2,1,0:T(8,128)}, u32[]{:S(2)}) copy-start(f32[2,32,256]{2,1,0:T(8,128)} %get-tuple-element.6) | copy-start | bytes 196612

commit v6 on v5

--- a/solution.py
+++ b/solution.py
@@ -140,9 +140,11 @@
 
         @pl.loop(0, NB * NZ)
         def _(k, m=m):
-            @pl.when(jnp.logical_not(pick_self(m, k)))
+            to = (d + NZ // 2 + k) % (NB * NZ)
+
+            @pl.when(jnp.logical_not(pick_self(m, to)))
             def _():
-                pick_copy(m, k).start()
+                pick_copy(m, to).start()
 
     lanes_own = pl.ds(pl.multiple_of(z * LANES, LANES), LANES)
     pick_own = pltpu.make_async_copy(cand.at[c, :, lanes_own], picked.at[d, c], pick_r.at[d, c])

time: 79.4 us -> 78.8 us (level)
  no operation moved by 1% of the time
where the time goes in v6:
time: 78.8 us; the launch traced here: 78.6 us
  Pallas kernels  75.7 us (96%)
  other arithmetic  2.26 us (3%)
    pallas_call x1, Pallas kernels, on_device(): pl.pallas_call(kernel, out_shape=(jax.ShapeDtypeStruct((MATS, 64, 256), f...  75.7 us
    convert_element_type x1, other arithmetic, on_device(): return (update.astype(bf16), first, second)  1.59 us

profile of v6, /device:TPU:1, one launch (start us, length us, event | category | flops | bytes accessed | tf_op | source)
XLA Modules:
  0.0 78.6 jit_solution(18368369684008520752)
XLA Ops:
  0.6 75.7 %shard_map.85 = (f32[2,64,256]{2,1,0:T(8,128)}, f32[2,32,256]{2,1,0:T(8,128)}) custom-call(s32[2]{0:T(128)} %owners_hbm.1, bf16[2,8,128,256]{3,2,1,0:T(8,128)(2,1)} %bitcast.4, bf16[2,64,1024]{2,1,0:T(8,128)(2,1)} %c_hbm.1, bf16[2,16,1024]{2,1,0:T(8,128)(2,1)} %bitcast.5, f32[2,32,256]{2,1,0:T(8,128)} %first_hbm.1, f32[2,32,256]{2,1,0:T(8,128)} %second_hbm.1), custom_call_target="tpu_custom_call" | custom-call | tf_op jit(solution)/shard_map/pallas_call | solution.py:499
  76.3 0.0 copy-start
  76.3 0.0 copy-start.1
  76.4 0.0 copy-start.2
  76.4 1.6 %convert_element_type.3 = bf16[2,64,256]{2,1,0:T(8,128)(2,1)} convert(f32[2,64,256]{2,1,0:T(8,128)} %get-tuple-element.5) | non-fusion elementwise | flops 32768 | bytes 196608 | tf_op jit(solution)/shard_map/convert_element_type | solution.py:555
  78.0 0.0 copy-done
  78.0 0.0 copy-done.1
  78.0 0.0 copy-done.2
  78.0 0.7 fusion
Async XLA Ops:
  76.3 1.6 %copy-start = (f32[2,32,256]{2,1,0:T(8,128)S(1)}, f32[2,32,256]{2,1,0:T(8,128)}, u32[]{:S(2)}) copy-start(f32[2,32,256]{2,1,0:T(8,128)} %first_hbm.1) | copy-start | bytes 196612
  76.3 1.6 %copy-start.1 = (f32[2,32,256]{2,1,0:T(8,128)S(1)}, f32[2,32,256]{2,1,0:T(8,128)}, u32[]{:S(2)}) copy-start(f32[2,32,256]{2,1,0:T(8,128)} %second_hbm.1) | copy-start | bytes 196612
  76.4 1.6 %copy-start.2 = (f32[2,32,256]{2,1,0:T(8,128)S(1)}, f32[2,32,256]{2,1,0:T(8,128)}, u32[]{:S(2)}) copy-start(f32[2,32,256]{2,1,0:T(8,128)} %get-tuple-element.6) | copy-start | bytes 196612

commit v7 on v6

--- a/solution.py
+++ b/solution.py
@@ -136,14 +136,13 @@
     def pick_self(m, k):
         return jnp.logical_and(c == m, k == d)
 
-    for m in range(MATS):
-
-        @pl.loop(0, NB * NZ)
-        def _(k, m=m):
-            to = (d + NZ // 2 + k) % (NB * NZ)
+    @pl.loop(0, NB * NZ)
+    def _(k):
+        to = (d + NZ // 2 + k) % (NB * NZ)
+        for m in range(MATS):
 
             @pl.when(jnp.logical_not(pick_self(m, to)))
-            def _():
+            def _(m=m):
                 pick_copy(m, to).start()
 
     lanes_own = pl.ds(pl.multiple_of(z * LANES, LANES), LANES)

time: 78.8 us -> 79.1 us (level)
  no operation moved by 1% of the time
where the time goes in v7:
time: 79.1 us; the launch traced here: 79 us
  Pallas kernels  76 us (96%)
  other arithmetic  2.26 us (3%)
    pallas_call x1, Pallas kernels, on_device(): pl.pallas_call(kernel, out_shape=(jax.ShapeDtypeStruct((MATS, 64, 256), f...  76 us
    convert_element_type x1, other arithmetic, on_device(): return (update.astype(bf16), first, second)  1.59 us

profile of v7, /device:TPU:1, one launch (start us, length us, event | category | flops | bytes accessed | tf_op | source)
XLA Modules:
  0.0 79.0 jit_solution(12822703216320842294)
XLA Ops:
  0.6 76.0 %shard_map.85 = (f32[2,64,256]{2,1,0:T(8,128)}, f32[2,32,256]{2,1,0:T(8,128)}) custom-call(s32[2]{0:T(128)} %owners_hbm.1, bf16[2,8,128,256]{3,2,1,0:T(8,128)(2,1)} %bitcast.4, bf16[2,64,1024]{2,1,0:T(8,128)(2,1)} %c_hbm.1, bf16[2,16,1024]{2,1,0:T(8,128)(2,1)} %bitcast.5, f32[2,32,256]{2,1,0:T(8,128)} %first_hbm.1, f32[2,32,256]{2,1,0:T(8,128)} %second_hbm.1), custom_call_target="tpu_custom_call" | custom-call | tf_op jit(solution)/shard_map/pallas_call | solution.py:498
  76.7 0.0 copy-start
  76.7 0.0 copy-start.1
  76.7 0.0 copy-start.2
  76.7 1.6 %convert_element_type.3 = bf16[2,64,256]{2,1,0:T(8,128)(2,1)} convert(f32[2,64,256]{2,1,0:T(8,128)} %get-tuple-element.5) | non-fusion elementwise | flops 32768 | bytes 196608 | tf_op jit(solution)/shard_map/convert_element_type | solution.py:554
  78.3 0.0 copy-done
  78.3 0.0 copy-done.1
  78.3 0.0 copy-done.2
  78.3 0.7 fusion
Async XLA Ops:
  76.7 1.6 %copy-start = (f32[2,32,256]{2,1,0:T(8,128)S(1)}, f32[2,32,256]{2,1,0:T(8,128)}, u32[]{:S(2)}) copy-start(f32[2,32,256]{2,1,0:T(8,128)} %first_hbm.1) | copy-start | bytes 196612
  76.7 1.6 %copy-start.1 = (f32[2,32,256]{2,1,0:T(8,128)S(1)}, f32[2,32,256]{2,1,0:T(8,128)}, u32[]{:S(2)}) copy-start(f32[2,32,256]{2,1,0:T(8,128)} %second_hbm.1) | copy-start | bytes 196612
  76.7 1.6 %copy-start.2 = (f32[2,32,256]{2,1,0:T(8,128)S(1)}, f32[2,32,256]{2,1,0:T(8,128)}, u32[]{:S(2)}) copy-start(f32[2,32,256]{2,1,0:T(8,128)} %get-tuple-element.6) | copy-start | bytes 196612
